TPU v7x, 128 devices: a whole 4x4x4 slice. The times are simulated.
128 devices in a mesh: clip: 4 (over x), seq: 32 (over y, z, core).
Axes of the slice: x: 4, y: 4, z: 4, core: 2. Of those that a mesh axis runs over, the one named last changes fastest.
Arguments:
- queries: bfloat16 [65536, 1024], P(('clip', 'seq')), parts along dimension 0, may hold values from -50 to 50
- rgb_kv: bfloat16 [8, 16384, 1024], P('clip', 'seq'), parts along dimension 0, may hold values from -16 to 16
- tile_ids: int32 [512, 8], P(('clip', 'seq')), parts along dimension 0, may hold values from 0 to 127, as said below
- tile_count: int32 [512], P(('clip', 'seq')), parts along dimension 0, may hold values from 2 to 8
- out_weight: bfloat16 [1024, 1024], replicated, may hold values from -0.1875 to 0.1875
- out_grad: bfloat16 [65536, 1024], P(('clip', 'seq')), parts along dimension 0, may hold values from -6 to 6
Outputs:
- joined: bfloat16 [65536, 1024], P(('clip', 'seq')), parts along dimension 0
- d_queries: bfloat16 [65536, 1024], P(('clip', 'seq')), parts along dimension 0
- d_kv: bfloat16 [8, 16384, 1024], P('clip', 'seq'), parts along dimension 0
- d_out_weight: float32 [4096, 1024], P(('clip', 'seq')), parts along dimension 0
There are 4 independent parts, one for each index of `clip`. A program takes and returns all parts, laid end to end along the dimension named above; an argument that names none is the same for every part. Nothing has to cross between parts.
Inputs may be any that keep to these rules, and one draw needn't show every extreme that they name: `tile_ids`: the 4 consecutive blocks of one group name, in their live entries, at most one distinct tile among tiles 4 s to 4 s + 3, for every s. The entries of one list name distinct tiles.
All inputs are finite; a program needn't handle non-finite values.
Results may differ from a plain program's by a relative error of at most 0.015.
Values may be sent and summed in bfloat16 or wider, within the bound.
No kernel may reach another device: no remote copies, remote signals or barrier semaphores. Data moves between devices by JAX's collectives and lax.ppermute only.
A program may use at most 192 MiB of HBM per device.

v0:
```python
import jax
import jax.numpy as jnp
from jax import lax
from jax.sharding import PartitionSpec as P

D = 1024
HEADS = 16
EB = 128
TILE = 128


masked_score = -1e30


def entry_tables(tile_ids, tile_count, tiles_dev, sources):
    entries = tile_ids.shape[1]
    source = tile_ids // tiles_dev
    within = tile_ids % tiles_dev
    usable = jnp.arange(entries)[None, :] < tile_count[:, None]
    matches = (source[:, :, None] == jnp.arange(sources)[None, None, :]) & usable[:, :, None]
    needed = jnp.any(matches, axis=(0, 1))
    wanted = jnp.max(jnp.where(matches, within[:, :, None], 0), axis=(0, 1))
    request = jnp.where(needed, wanted, -1)
    return (source, usable, request)


def entry_rows(slot_rows, source, position):
    chosen = lax.dynamic_index_in_dim(source, position, 1, keepdims=False)
    picked = jnp.take(slot_rows, chosen, axis=0)
    return picked.reshape(picked.shape[0], picked.shape[1], HEADS, D // HEADS)


def entry_scores(query_heads, key_rows, usable, position, score_scale):
    logits = (
        jnp.einsum("bqhe,bthe->bhqt", query_heads, key_rows, preferred_element_type=jnp.float32)
        * score_scale
    )
    usable_now = lax.dynamic_index_in_dim(usable, position, 1, keepdims=False)
    return jnp.where(usable_now[:, None, None, None], logits, masked_score)


def local(queries, rgb_kv, tile_ids, tile_count, out_weight, out_grad):
    sources = lax.axis_size("seq")
    blocks = tile_ids.shape[0]
    tiles_dev = rgb_kv.shape[1] // TILE
    head_dim = D // HEADS
    score_scale = head_dim ** (-0.5)
    source, usable, request = entry_tables(tile_ids, tile_count, tiles_dev, sources)
    asked_for = lax.all_to_all(request[:, None], "seq", split_axis=0, concat_axis=0, tiled=True)[
        :, 0
    ]
    own_tiles = rgb_kv.reshape(2, tiles_dev, TILE, D)
    outgoing = jnp.take(own_tiles, jnp.maximum(asked_for, 0), axis=1)
    query_heads = queries.reshape(blocks, EB, HEADS, head_dim)
    trip_count = tile_ids.shape[1]
    fetched = lax.all_to_all(outgoing, "seq", split_axis=1, concat_axis=1, tiled=True)
    key_slots = fetched[0]
    value_slots = fetched[1]

    def stats_step(position, state_pair):
        run_max, run_sum = state_pair
        logits = entry_scores(
            query_heads, entry_rows(key_slots, source, position), usable, position, score_scale
        )
        new_max = jnp.maximum(run_max, jnp.max(logits, axis=3))
        run_sum = run_sum * jnp.exp(run_max - new_max) + jnp.sum(
            jnp.exp(logits - new_max[..., None]), axis=3
        )
        return (new_max, run_sum)

    start_max = jnp.full((blocks, HEADS, EB), masked_score, jnp.float32)
    row_max, row_sum = lax.fori_loop(
        0, trip_count, stats_step, (start_max, jnp.zeros_like(start_max))
    )

    def probabilities(logits):
        return jnp.exp(logits - row_max[..., None]) / row_sum[..., None]

    def output_step(position, running):
        key_rows = entry_rows(key_slots, source, position)
        value_rows = entry_rows(value_slots, source, position)
        weights = probabilities(
            entry_scores(query_heads, key_rows, usable, position, score_scale)
        ).astype(jnp.bfloat16)
        return running + jnp.einsum(
            "bhqt,bthe->bqhe", weights, value_rows, preferred_element_type=jnp.float32
        )

    attended_full = lax.fori_loop(
        0, trip_count, output_step, jnp.zeros(query_heads.shape, jnp.float32)
    )
    attended = attended_full.astype(jnp.bfloat16).reshape(queries.shape)
    joined_out = jnp.dot(attended, out_weight, preferred_element_type=jnp.float32).astype(
        jnp.bfloat16
    )
    d_attended = lax.dot_general(
        out_grad, out_weight, (((1,), (1,)), ((), ())), preferred_element_type=jnp.float32
    ).astype(jnp.bfloat16)
    d_out_weight = lax.psum_scatter(
        lax.dot_general(
            attended, out_grad, (((0,), (0,)), ((), ())), preferred_element_type=jnp.float32
        ).astype(jnp.bfloat16),
        "seq",
        scatter_dimension=0,
        tiled=True,
    ).astype(jnp.float32)
    d_heads = d_attended.reshape(query_heads.shape)
    delta_rows = jnp.sum(d_heads.astype(jnp.float32) * attended_full, axis=3).transpose(0, 2, 1)

    def grad_step(position, state_pair):
        d_query_sum, grads_both = state_pair
        key_rows = entry_rows(key_slots, source, position)
        value_rows = entry_rows(value_slots, source, position)
        probability = probabilities(
            entry_scores(query_heads, key_rows, usable, position, score_scale)
        )
        weights = probability.astype(jnp.bfloat16)
        d_weights = jnp.einsum(
            "bqhe,bthe->bhqt", d_heads, value_rows, preferred_element_type=jnp.float32
        )
        d_scores = (probability * (d_weights - delta_rows[..., None])).astype(jnp.bfloat16)
        d_query_sum = (
            d_query_sum
            + jnp.einsum("bhqt,bthe->bqhe", d_scores, key_rows, preferred_element_type=jnp.float32)
            * score_scale
        )
        usable_now = lax.dynamic_index_in_dim(usable, position, 1, keepdims=False).astype(
            jnp.float32
        )[:, None, None]
        d_keys = jnp.einsum(
            "bhqt,bqhe->bthe", d_scores, query_heads, preferred_element_type=jnp.float32
        ).reshape(blocks, TILE, D) * (score_scale * usable_now)
        d_values = (
            jnp.einsum(
                "bhqt,bqhe->bthe", weights, d_heads, preferred_element_type=jnp.float32
            ).reshape(blocks, TILE, D)
            * usable_now
        )
        chosen = lax.dynamic_index_in_dim(source, position, 1, keepdims=False)
        grads_both = grads_both.at[0, chosen].add(d_keys).at[1, chosen].add(d_values)
        return (d_query_sum, grads_both)

    start_grads = jnp.zeros((2, sources, TILE, D), jnp.float32)
    d_query_sum, grads_both = lax.fori_loop(
        0, trip_count, grad_step, (jnp.zeros(query_heads.shape, jnp.float32), start_grads)
    )
    d_queries = d_query_sum.reshape(queries.shape).astype(jnp.bfloat16)
    returned = lax.all_to_all(
        grads_both.astype(jnp.bfloat16), "seq", split_axis=1, concat_axis=1, tiled=True
    )
    owner_pick = (asked_for[:, None] == jnp.arange(tiles_dev)[None, :]).astype(jnp.bfloat16)
    tile_grads = jnp.einsum(
        "rl,crtd->cltd", owner_pick, returned, preferred_element_type=jnp.float32
    )
    d_kv = tile_grads.reshape(2, tiles_dev * TILE, D).astype(jnp.bfloat16)
    return (joined_out, d_queries, d_kv, d_out_weight)


def solution(mesh):
    placed = (
        P(("clip", "seq"), None),
        P("clip", "seq", None),
        P(("clip", "seq"), None),
        P(("clip", "seq")),
        P(),
        P(("clip", "seq"), None),
    )
    return jax.shard_map(
        local,
        mesh=mesh,
        in_specs=placed,
        out_specs=(
            P(("clip", "seq"), None),
            P(("clip", "seq"), None),
            P("clip", "seq", None),
            P(("clip", "seq"), None),
        ),
        check_vma=False,
    )
```

profile of v0, /device:TPU:50, one launch (start us, length us, event | category | flops | bytes accessed | tf_op | source)
XLA Modules:
  0.0 1226.8 jit_solution(15206718256814219377)
XLA Ops:
  9.3 12.2 all_to_all.19
  23.3 7.1 gather_fusion.5
  30.4 14.2 %select_bitcast_fusion.2 = bf16[2,32,128,1024]{3,2,0,1:T(8,128)(2,1)} fusion(bf16[32,2,128,1024]{3,2,1,0:T(8,128)(2,1)} %gather_fusion.5, pred[32]{0:T(512)(128)(4,1)S(1)} %maximum_compare_fusion), kind=kLoop, calls=%fused_computation.55 | loop fusion | flops 8388608 | bytes 33554464 | tf_op jit(solution)/shard_map/jit(_take)/select_n | solution.py:53
  44.6 8.7 all-to-all-start.1
  64.0 258.2 %all-to-all-done.1 = bf16[2,32,128,1024]{3,2,0,1:T(8,128)(2,1)} async-done(((bf16[2,32,128,1024]{3,2,0,1:T(8,128)(2,1)}), bf16[2,32,128,1024]{3,2,0,1:T(8,128)(2,1)}, u32[]{:S(2)}, u32[]{:S(2)}) %all-to-all-start.1) | async-done | bytes 16777248 | tf_op jit(solution)/shard_map/all_to_all | solution.py:56
  322.2 11.9 slice_bitcast_fusion
  334.1 58.9 %while.46 = (s32[]{:T(128)}, f32[4,16,128]{2,1,0:T(8,128)S(1)}, f32[4,16,128]{2,1,0:T(8,128)S(1)}, pred[4,8]{0,1:T(8,128)(4,1)S(1)}, s32[4,8]{0,1:T(8,128)S(1)},...) while((s32[]{:T(128)}, f32[4,16,128]{2,1,0:T(8,128)S(1)}, ...), condition=%wide.region_5.7_spmd.clone, body=%wide.region_2.6_spmd.clone.sunk | while | flops 142124064 | bytes 17207504 | solution.py:72
  393.0 143.3 %while.47 = (s32[]{:T(128)}, f32[4,128,16,64]{1,3,2,0:T(8,128)}, s32[4,8]{0,1:T(8,128)S(1)}, bf16[32,128,1024]{2,1,0:T(8,128)(2,1)}, pred[4,8]{0,1:T(8,128)(4,1)...) while((s32[]{:T(128)}, f32[4,128,16,64]{1,3,2,0:T(8,128)}, ...), condition=%wide.region_7.9_spmd.clone, body=%wide.region_6.8_spmd.clone.sunk | while | flops 275776544 | bytes 19992812 | solution.py:89
  422.4 5.2 bitcast_add_fusion.4
  440.6 5.2 bitcast_add_fusion.4
  458.7 5.2 bitcast_add_fusion.4
  476.8 5.2 bitcast_add_fusion.4
  494.9 5.2 bitcast_add_fusion.4
  513.0 5.2 bitcast_add_fusion.4
  531.1 5.2 bitcast_add_fusion.4
  540.4 11.7 broadcast_in_dim.169
  552.1 359.6 %while.48 = (s32[]{:T(128)}, f32[4,128,16,64]{1,3,2,0:T(8,128)}, f32[2,32,128,1024]{3,2,1,0:T(8,128)}, s32[4,8]{0,1:T(8,128)S(1)}, bf16[32,128,1024]{2,1,0:T(8,1...) while((s32[]{:T(128)}, f32[4,128,16,64]{1,3,2,0:T(8,128)}, ...), condition=%wide.region_12.14_spmd.clone, body=%wide.region_9.13_spmd.clone.sunk | while | flops 684196928 | bytes 101814880 | solution.py:144
  631.5 5.1 scatter_fusion
  722.0 5.1 scatter_fusion
  911.7 17.5 %copy.185 = bf16[2,32,128,1024]{3,2,0,1:T(8,128)(2,1)} copy(f32[2,32,128,1024]{3,2,1,0:T(8,128)} %get-tuple-element.488) | data formatting | bytes 50331648 | tf_op jit(solution)/shard_map/while | solution.py:144
  929.3 6.1 all-to-all-start.2
  949.2 201.7 %reduce-scatter.2.cloned.1.call-done = bf16[32,1024]{1,0:T(8,128)(2,1)} async-done(((bf16[1024,1024]{1,0:T(8,128)(2,1)}), bf16[32,1024]{1,0:T(8,128)(2,1)}) %reduce-scatter.2.cloned.1.call-update) | async-done | bytes 65552 | tf_op jit(solution)/shard_map/reduce_scatter | solution.py:99
  1152.5 49.9 %all-to-all-done.2 = bf16[2,32,128,1024]{3,2,0,1:T(8,128)(2,1)} async-done(((bf16[2,32,128,1024]{3,2,0,1:T(8,128)(2,1)}), bf16[2,32,128,1024]{3,2,0,1:T(8,128)(2,1)}, u32[]{:S(2)}, u32[]{:S(2)}) %all-to-all-start.2) | async-done | bytes 16777248 | tf_op jit(solution)/shard_map/all_to_all | solution.py:148
  1202.4 15.4 %convert_bitcast_fusion = bf16[2,4,128,1024]{3,1,2,0:T(4,128)(2,1)S(1)} fusion(bf16[2,32,128,1024]{3,2,0,1:T(8,128)(2,1)} %all-to-all-done.2, s32[32]{0:T(128)S(1)} %copy-done.13), kind=kOutput, calls=%fused_computation.60 | convolution fusion | flops 68157568 | bytes 18874496 | tf_op jit(solution)/shard_map/rl,crtd->cltd/dot_general | solution.py:152
  (465 shorter events, 549.2 us)
Async XLA Ops:
  7.2 16.2 %copy-start = (bf16[2,512,1024]{2,1,0:T(8,128)(2,1)S(1)}, bf16[2,512,1024]{2,1,0:T(8,128)(2,1)}, u32[]{:S(2)}) copy-start(bf16[2,512,1024]{2,1,0:T(8,128)(2,1)} %param.15) | copy-start | bytes 6291460
  44.6 8.7 copy-start.10
  44.6 8.7 copy-start.14
  44.6 277.5 %all-to-all-start.1 = ((bf16[2,32,128,1024]{3,2,0,1:T(8,128)(2,1)}), bf16[2,32,128,1024]{3,2,0,1:T(8,128)(2,1)}, u32[]{:S(2)}, u32[]{:S(2)}) async-start(bf16[2,32,128,1024]{3,2,0,1:T(8,128)(2,1)} %select_bitcast_fusion.2), calls=%async_computation.1 | async-start | bytes 33554432 | tf_op jit(solution)/shard_map/all_to_all | solution.py:56
  57.5 6.5 copy-start.7
  574.3 3.4 copy-start.5
  586.4 5.0 copy-start.2
  631.5 5.1 copy-start.2
  663.0 3.4 copy-start.5
  676.7 5.1 copy-start.2
  708.3 3.4 copy-start.5
  722.0 5.1 copy-start.2
  753.5 3.4 copy-start.5
  767.2 5.1 copy-start.2
  812.4 5.0 copy-start.2
  843.8 3.4 copy-start.5
  857.5 5.1 copy-start.2
  889.0 3.4 copy-start.5
  902.7 4.9 copy-start.2
  929.3 6.1 copy-start.8
  929.3 273.1 %all-to-all-start.2 = ((bf16[2,32,128,1024]{3,2,0,1:T(8,128)(2,1)}), bf16[2,32,128,1024]{3,2,0,1:T(8,128)(2,1)}, u32[]{:S(2)}, u32[]{:S(2)}) async-start(bf16[2,32,128,1024]{3,2,0,1:T(8,128)(2,1)} %copy.185), calls=%async_computation.2 | async-start | bytes 33554432 | tf_op jit(solution)/shard_map/all_to_all | solution.py:148
  935.3 215.6 %reduce-scatter.2.cloned.1.call-start = ((), (), s32[]{:S(2)}) async-start(), calls=%async_computation.4 | async-start | bytes 2162688 | tf_op jit(solution)/shard_map/reduce_scatter | solution.py:99
  942.6 259.8 %copy-start.13 = (s32[32]{0:T(128)S(1)}, s32[32]{0:T(128)}, u32[]{:S(2)}) copy-start(s32[32]{0:T(128)} %copy-done.12) | copy-start | bytes 388
  1202.4 17.4 %copy-start.1 = (bf16[2,512,1024]{2,1,0:T(8,128)(2,1)S(1)}, bf16[2,512,1024]{2,1,0:T(8,128)(2,1)}, u32[]{:S(2)}) copy-start(bf16[2,512,1024]{2,1,0:T(8,128)(2,1)} %param.15) | copy-start | bytes 6291460
  (30 other events, 59.0 us)
Sparse Core Ops, SparseCore 0:
  940.3 210.6 reduce-scatter.1
where the time goes:
time: 1230 us
  waiting for transfers between devices  510 us (41%)
  local copies, waits for them, and re-layouts  330 us (27%)
  other arithmetic  178 us (14%)
  matrix products  166 us (13%)
  starting transfers between devices  14.8 us (1%)
  between operations  14.5 us (1%)
    all_to_all x1, waiting for transfers between devices, local(): lax.all_to_all(outgoing, 'seq', split_axis=1, concat_axis=1, tiled=True)  258 us
    reduce_scatter x1, waiting for transfers between devices, local(): lax.psum_scatter(lax.dot_general(attended, out_grad, (((0,), (0,)), ((),...  202 us
    gather x40, local copies, waits for them, and re-layouts, entry_rows(): picked = jnp.take(slot_rows, chosen, axis=0)  160 us
    scatter-add x16, other arithmetic, grad_step(): grads_both.at[0, chosen].add(d_keys).at[1, chosen].add(d_values)  74.3 us
    select_n x40, local copies, waits for them, and re-layouts, entry_rows(): picked = jnp.take(slot_rows, chosen, axis=0)  64.9 us
    all_to_all x1, waiting for transfers between devices, local(): lax.all_to_all(grads_both.astype(jnp.bfloat16), 'seq', split_axis=1, conc...  49.9 us
    dot_general x8, matrix products, output_step(): jnp.einsum('bhqt,bthe->bqhe', weights, value_rows, preferred_element_type...  40.2 us
    dot_general x8, matrix products, grad_step(): jnp.einsum('bhqt,bthe->bqhe', d_scores, key_rows, preferred_element_type=...  27.7 us
  transfers between devices with their start and end apart: 3, of which 3 were waited for; matrix products, arithmetic and copies ran while one was open for 2% of the time, Pallas kernels for 0%

commit v1 on v0

v1 whole, which is shorter than its diff:
```python
import functools

import jax
import jax.numpy as jnp
from jax import lax
from jax.experimental import pallas as pl
from jax.experimental.pallas import tpu as pltpu
from jax.sharding import PartitionSpec as P


D = 1024
HEADS = 16
EB = 128
TILE = 128
HEAD_DIM = D // HEADS
SCALE = HEAD_DIM ** -0.5
PAIR = 2 * HEAD_DIM
CHUNKS = 4
COLS = D // CHUNKS
NY, NZ, NCORE = 4, 4, 2
LOCAL = 4
DESTS = 8
masked_score = -1e30
ROWS = [[y * NZ * NCORE + i for i in range(NZ * NCORE)] for y in range(NY)]
COLUMNS = [
    [(y * NZ + z) * NCORE + c for y in range(NY) for c in range(NCORE)] for z in range(NZ)
]


def shift(dy, dz, dc):
    pairs = []
    for y in range(NY):
        for z in range(NZ):
            for c in range(NCORE):
                to = (((y + dy) % NY) * NZ + (z + dz) % NZ) * NCORE + (c ^ dc)
                pairs.append(((y * NZ + z) * NCORE + c, to))
    return pairs


def move(x, dy, dz, dc):
    if dy % NY == 0 and dz % NZ == 0 and dc == 0:
        return x
    return lax.ppermute(x, "seq", shift(dy, dz, dc))


def dot(a, b, ca, cb):
    return lax.dot_general(a, b, (((ca,), (cb,)), ((), ())), preferred_element_type=jnp.float32)


def pack_kernel(index_ref, *refs):
    held, packed, sem = refs[:4], refs[4:12], refs[12]
    copies = []
    for d in range(DESTS):
        for k in range(4):
            copy = pltpu.make_async_copy(
                held[k].at[:, index_ref[d, k]], packed[d].at[:, k], sem.at[d, k]
            )
            copy.start()
            copies.append(copy)
    for copy in copies:
        copy.wait()


def pack(index, held):
    shape = jax.ShapeDtypeStruct((2, 4, TILE, COLS), jnp.bfloat16)
    return pl.pallas_call(
        pack_kernel,
        grid_spec=pltpu.PrefetchScalarGridSpec(
            num_scalar_prefetch=1,
            grid=(1,),
            in_specs=[pl.BlockSpec((2, LOCAL, TILE, COLS), lambda i, index: (0, 0, 0, 0))] * 4,
            out_specs=[pl.BlockSpec(memory_space=pl.ANY)] * DESTS,
            scratch_shapes=[pltpu.SemaphoreType.DMA((DESTS, 4))],
        ),
        out_shape=[shape] * DESTS,
        name="pack",
    )(index, *held)


def merge_kernel(index_ref, *refs):
    parts, sums, acc = refs[:8], refs[8:12], refs[12]
    for k in range(4):
        acc[...] = jnp.zeros_like(acc)
        for d in range(DESTS):
            tile = index_ref[d, k]

            @pl.when(tile >= 0)
            def _():
                acc[tile] += parts[d][0, k].astype(jnp.float32)

        sums[k][0] = acc[...].astype(jnp.bfloat16)


def merge(index, parts):
    block = pl.BlockSpec((1, 4, TILE, COLS), lambda i, index: (i, 0, 0, 0))
    shape = jax.ShapeDtypeStruct((2, 4, TILE, COLS), jnp.bfloat16)
    return pl.pallas_call(
        merge_kernel,
        grid_spec=pltpu.PrefetchScalarGridSpec(
            num_scalar_prefetch=1,
            grid=(2,),
            in_specs=[block] * DESTS,
            out_specs=[block] * 4,
            scratch_shapes=[pltpu.VMEM((LOCAL, TILE, COLS), jnp.float32)],
        ),
        out_shape=[shape] * 4,
        name="merge",
    )(index, *parts)


def attention_kernel(blocks, slot_ref, count_ref, q_ref, do_ref, *refs):
    tiles = refs[:8]
    o_ref, dq_ref = refs[8:10]
    grads = refs[10:18]
    keys, values, d_keys, d_values, query2, d_out2, scores, sums = refs[18:]
    for d in range(DESTS):
        for k in range(4):
            keys[4 * d + k] = tiles[d][0, k]
            values[4 * d + k] = tiles[d][1, k]
    d_keys[...] = jnp.zeros_like(d_keys)
    d_values[...] = jnp.zeros_like(d_values)
    first = lax.broadcasted_iota(jnp.int32, (EB, PAIR), 1) < HEAD_DIM
    zero = jnp.zeros((EB, PAIR), jnp.bfloat16)
    trips = count_ref[0]
    for b in range(blocks):
        rows = slice(b * EB, (b + 1) * EB)
        query = q_ref[rows, :] * jnp.bfloat16(SCALE)
        query2[b, :EB, :] = jnp.where(first, query, zero)
        query2[b, EB:, :] = jnp.where(first, zero, query)
        d_out = do_ref[rows, :]
        d_out2[b, :EB, :] = jnp.where(first, d_out, zero)
        d_out2[b, EB:, :] = jnp.where(first, zero, d_out)
        trips = jnp.maximum(trips, count_ref[b])

    def score_step(j, maxima):
        updated = []
        for b in range(blocks):
            logits = dot(keys[slot_ref[b, j]], query2[b], 1, 1)
            logits = jnp.where(j < count_ref[b], logits, masked_score)
            scores[b, j] = logits
            updated.append(
                jnp.maximum(maxima[b], jnp.max(logits.reshape(TILE // 8, 8, 2 * EB), axis=0))
            )
        return tuple(updated)

    maxima = lax.fori_loop(
        0, trips, score_step, (jnp.full((8, 2 * EB), masked_score, jnp.float32),) * blocks
    )
    row_max = [jnp.max(m, axis=0, keepdims=True) for m in maxima]
    sums[...] = jnp.zeros_like(sums)

    def output_step(j, totals):
        updated = []
        for b in range(blocks):
            weight = jnp.exp(scores[b, j] - row_max[b])
            scores[b, j] = weight
            updated.append(totals[b] + jnp.sum(weight.reshape(TILE // 8, 8, 2 * EB), axis=0))
            sums[b] += dot(values[slot_ref[b, j]], weight.astype(jnp.bfloat16), 0, 0)
        return tuple(updated)

    totals = lax.fori_loop(
        0, trips, output_step, (jnp.zeros((8, 2 * EB), jnp.float32),) * blocks
    )
    inverse = [1.0 / jnp.sum(t, axis=0, keepdims=True) for t in totals]
    delta = []
    for b in range(blocks):
        rows = slice(b * EB, (b + 1) * EB)
        out2 = sums[b] * inverse[b]
        out = jnp.concatenate([out2[:HEAD_DIM, :EB], out2[HEAD_DIM:, EB:]], axis=0)
        product = out * do_ref[rows, :].astype(jnp.float32).T
        delta.append(
            jnp.concatenate(
                [
                    jnp.sum(product[:HEAD_DIM], axis=0, keepdims=True),
                    jnp.sum(product[HEAD_DIM:], axis=0, keepdims=True),
                ],
                axis=1,
            )
        )
        o_ref[rows, :] = out.T.astype(jnp.bfloat16)
    sums[...] = jnp.zeros_like(sums)

    def grad_step(j, carry):
        for b in range(blocks):
            slot = slot_ref[b, j]
            weight = scores[b, j] * inverse[b]
            d_weight = dot(values[slot], d_out2[b], 1, 1)
            d_score = (weight * (d_weight - delta[b])).astype(jnp.bfloat16)
            d_values[slot] += dot(weight.astype(jnp.bfloat16), d_out2[b], 1, 0)
            d_keys[slot] += dot(d_score, query2[b], 1, 0)
            sums[b] += dot(keys[slot], d_score, 0, 0)
        return carry

    lax.fori_loop(0, trips, grad_step, 0)
    for b in range(blocks):
        d_query2 = sums[b]
        d_query = jnp.concatenate(
            [d_query2[:HEAD_DIM, :EB], d_query2[HEAD_DIM:, EB:]], axis=0
        )
        dq_ref[b * EB : (b + 1) * EB, :] = (d_query.T * SCALE).astype(jnp.bfloat16)
    for d in range(DESTS):
        for k in range(4):
            grads[d][0, k] = d_keys[4 * d + k].astype(jnp.bfloat16)
            grads[d][1, k] = d_values[4 * d + k].astype(jnp.bfloat16)


def attention(chunk, slots, counts, queries, d_attended, tiles):
    tokens = queries.shape[0]
    blocks = tokens // EB
    entries = slots.shape[1]
    pairs = COLS // PAIR
    wide = pl.BlockSpec((tokens, PAIR), lambda p, s, c: (0, chunk * pairs + p))
    own = pl.BlockSpec((tokens, PAIR), lambda p, s, c: (0, p))
    tile = pl.BlockSpec((2, 4, TILE, PAIR), lambda p, s, c: (0, 0, 0, p))
    out = jax.ShapeDtypeStruct((tokens, COLS), jnp.bfloat16)
    grad = jax.ShapeDtypeStruct((2, 4, TILE, COLS), jnp.bfloat16)
    work = DESTS * 4
    results = pl.pallas_call(
        functools.partial(attention_kernel, blocks),
        grid_spec=pltpu.PrefetchScalarGridSpec(
            num_scalar_prefetch=2,
            grid=(pairs,),
            in_specs=[wide, wide] + [tile] * DESTS,
            out_specs=[own, own] + [tile] * DESTS,
            scratch_shapes=[
                pltpu.VMEM((work, TILE, PAIR), jnp.bfloat16),
                pltpu.VMEM((work, TILE, PAIR), jnp.bfloat16),
                pltpu.VMEM((work, TILE, PAIR), jnp.float32),
                pltpu.VMEM((work, TILE, PAIR), jnp.float32),
                pltpu.VMEM((blocks, 2 * EB, PAIR), jnp.bfloat16),
                pltpu.VMEM((blocks, 2 * EB, PAIR), jnp.bfloat16),
                pltpu.VMEM((blocks, entries, TILE, 2 * EB), jnp.float32),
                pltpu.VMEM((blocks, PAIR, 2 * EB), jnp.float32),
            ],
        ),
        out_shape=[out, out] + [grad] * DESTS,
        cost_estimate=pl.CostEstimate(
            flops=12 * pairs * blocks * entries * TILE * 2 * EB * PAIR,
            transcendentals=pairs * blocks * entries * TILE * 2 * EB,
            bytes_accessed=4 * work * TILE * COLS * 2,
        ),
        compiler_params=pltpu.CompilerParams(vmem_limit_bytes=56 * 1024 * 1024),
        name="attention",
    )(slots, counts, queries, d_attended, *tiles)
    return results[0], results[1], results[2:]


def local(queries, rgb_kv, tile_ids, tile_count, out_weight, out_grad):
    me = lax.axis_index("seq")
    y, z, c = me // (NZ * NCORE), (me // NCORE) % NZ, me % NCORE
    devices = NY * NZ * NCORE
    own_tiles = rgb_kv.reshape(2, LOCAL, TILE, D)
    source = tile_ids // LOCAL
    within = tile_ids % LOCAL
    usable = jnp.arange(tile_ids.shape[1])[None, :] < tile_count[:, None]
    matches = (source[:, :, None] == jnp.arange(devices)[None, None, :]) & usable[:, :, None]
    wanted = jnp.max(jnp.where(matches, within[:, :, None], -1), axis=(0, 1))
    told = [
        lax.all_to_all(
            operand, "seq", 0, 0, axis_index_groups=groups, tiled=True
        ).reshape(-1, NCORE, 4)
        for operand, groups in (
            (wanted.reshape(NY, NZ * NCORE).T, ROWS),
            (wanted.reshape(NY, NZ, NCORE).transpose(0, 2, 1).reshape(-1, NZ), COLUMNS),
        )
    ]
    source_y, source_z = source // (NZ * NCORE), (source // NCORE) % NZ
    flip = (source % NCORE) ^ c
    back_y, back_z = (y - source_y) % NY, (z - source_z) % NZ
    slots = (
        (back_z * NCORE + flip) * 4 + back_y,
        (back_y * NCORE + flip) * 4 + back_z,
    )
    far = jnp.arange(4)[:, None, None]
    core = c ^ jnp.arange(NCORE)[None, :, None]
    near = jnp.arange(4)[None, None, :]
    asked = (
        told[0][(z + far) % NZ, core, (y - near) % NY].reshape(DESTS, 4),
        told[1][(y + far) % NY, core, (z - near) % NZ].reshape(DESTS, 4),
    )

    d_attended = lax.dot_general(
        out_grad, out_weight, (((1,), (1,)), ((), ())), preferred_element_type=jnp.float32
    ).astype(jnp.bfloat16)

    attended, d_queries, d_kv = [], [], []
    for chunk in range(CHUNKS):
        along_y = chunk % 2 == 0
        kind = 0 if along_y else 1

        def near_move(x, k):
            return move(x, k, 0, 0) if along_y else move(x, 0, k, 0)

        def far_move(x, d, sign):
            step, core = sign * (d // NCORE), d % NCORE
            return move(x, 0, step, core) if along_y else move(x, step, 0, core)

        mine = own_tiles[..., chunk * COLS : (chunk + 1) * COLS]
        held = [near_move(mine, k) for k in range(4)]
        packed = pack(jnp.maximum(asked[kind], 0), held)
        tiles = [far_move(packed[d], d, 1) for d in range(DESTS)]
        out, d_query, grads = attention(chunk, slots[kind], tile_count, queries, d_attended, tiles)
        attended.append(out)
        d_queries.append(d_query)
        parts = [far_move(grads[d], d, -1) for d in range(DESTS)]
        sums = merge(asked[kind], parts)
        returned = [near_move(sums[k], -k) for k in range(4)]
        total = sum(r.astype(jnp.float32) for r in returned)
        d_kv.append(total.astype(jnp.bfloat16))
    attended = jnp.concatenate(attended, axis=1)
    joined = jnp.dot(attended, out_weight, preferred_element_type=jnp.float32).astype(jnp.bfloat16)
    product = lax.dot_general(
        attended, out_grad, (((0,), (0,)), ((), ())), preferred_element_type=jnp.float32
    ).astype(jnp.bfloat16)
    d_out_weight = lax.psum_scatter(
        product, "seq", scatter_dimension=0, tiled=True
    ).astype(jnp.float32)
    d_queries = jnp.concatenate(d_queries, axis=1)
    d_kv = jnp.concatenate(d_kv, axis=3).reshape(rgb_kv.shape)
    return (joined, d_queries, d_kv, d_out_weight)


def solution(mesh):
    placed = (
        P(("clip", "seq"), None),
        P("clip", "seq", None),
        P(("clip", "seq"), None),
        P(("clip", "seq")),
        P(),
        P(("clip", "seq"), None),
    )

    return jax.shard_map(
        local,
        mesh=mesh,
        in_specs=placed,
        out_specs=(
            P(("clip", "seq"), None),
            P(("clip", "seq"), None),
            P("clip", "seq", None),
            P(("clip", "seq"), None),
        ),
        check_vma=False,
    )
```

time: 1230 us -> 565 us (0.46)
  the two profiles are of different devices: /device:TPU:50 before, /device:TPU:7 now
where the time goes in v1:
time: 565 us; the launch traced here: 555 us
  starting transfers between devices  182 us (32%)
  waiting for transfers between devices  180 us (32%)
  Pallas kernels  143 us (25%)
  between operations  15.3 us (3%)
  local copies, waits for them, and re-layouts  12.4 us (2%)
  other arithmetic  11.7 us (2%)
  matrix products  11.1 us (2%)
    ppermute x80, waiting for transfers between devices, move(): return lax.ppermute(x, 'seq', shift(dy, dz, dc))  174 us
    ppermute x80, starting transfers between devices, move(): return lax.ppermute(x, 'seq', shift(dy, dz, dc))  172 us
    pallas_call x4, Pallas kernels, attention(): pl.pallas_call(functools.partial(attention_kernel, blocks), grid_spec=plt...  106 us
    pallas_call x4, Pallas kernels, pack(): pl.pallas_call(pack_kernel, grid_spec=pltpu.PrefetchScalarGridSpec(num_sc...  18.2 us
    pallas_call x4, Pallas kernels, merge(): pl.pallas_call(merge_kernel, grid_spec=pltpu.PrefetchScalarGridSpec(num_s...  18.1 us
  transfers between devices with their start and end apart: 83, of which 22 were waited for; matrix products, arithmetic and copies ran while one was open for 5% of the time, Pallas kernels for 26%

profile of v1, /device:TPU:7, one launch (start us, length us, event | category | flops | bytes accessed | tf_op | source)
XLA Modules:
  0.0 555.1 jit_solution(4534148808729581279)
XLA Ops:
  21.5 5.3 all-to-all-start
  29.5 7.3 %collective-permute-done.1.refs_2_ = bf16[2,4,128,256]{3,2,1,0:T(8,128)(2,1)} collective-permute-done((bf16[2,4,128,256]{3,2,1,0:T(8,128)(2,1)}, bf16[2,4,128,256]{3,2,1,0:T(8,128)(2,1)}, u32[]{:S(2)}, u32[]{:S(2)}) %collective-permute-start.1) | collective-permute-done | bytes 524320 | tf_op jit(solution)/shard_map/ppermute | solution.py:43
  51.6 9.7 %collective-permute-done.20.refs_1_ = bf16[2,4,128,256]{3,2,1,0:T(8,128)(2,1)} collective-permute-done((bf16[2,4,128,256]{3,2,1,0:T(8,128)(2,1)S(1)}, bf16[2,4,128,256]{3,2,1,0:T(8,128)(2,1)}, u32[]{:S(2)}, u32[]{:S(2)}) %collective-permute-start.20) | collective-permute-done | bytes 524320 | tf_op jit(solution)/shard_map/ppermute | solution.py:43
  78.9 4.7 pack.5
  90.7 26.0 %collective-permute-done.5.refs_3_ = bf16[2,4,128,256]{3,2,1,0:T(8,128)(2,1)} collective-permute-done((bf16[2,4,128,256]{3,2,1,0:T(8,128)(2,1)}, bf16[2,4,128,256]{3,2,1,0:T(8,128)(2,1)}, u32[]{:S(2)}, u32[]{:S(2)}) %collective-permute-start.5) | collective-permute-done | bytes 524320 | tf_op jit(solution)/shard_map/ppermute | solution.py:43
  121.9 10.8 %collective-permute-done.9.refs_7_ = bf16[2,4,128,256]{3,2,1,0:T(8,128)(2,1)S(1)} collective-permute-done((bf16[2,4,128,256]{3,2,1,0:T(8,128)(2,1)}, bf16[2,4,128,256]{3,2,1,0:T(8,128)(2,1)S(1)}, u32[]{:S(2)}, u32[]{:S(2)}) %collective-permute-start.9) | collective-permute-done | bytes 524320 | tf_op jit(solution)/shard_map/ppermute | solution.py:43
  141.3 24.4 %collective-permute-done.15.refs_3_ = bf16[2,4,128,256]{3,2,1,0:T(8,128)(2,1)} collective-permute-done((bf16[2,4,128,256]{3,2,1,0:T(8,128)(2,1)}, bf16[2,4,128,256]{3,2,1,0:T(8,128)(2,1)}, u32[]{:S(2)}, u32[]{:S(2)}) %collective-permute-start.15) | collective-permute-done | bytes 524320 | tf_op jit(solution)/shard_map/ppermute | solution.py:43
  165.9 4.6 collective-permute-start.26
  181.7 33.0 %collective-permute-done.25.refs_3_ = bf16[2,4,128,256]{3,2,1,0:T(8,128)(2,1)} collective-permute-done((bf16[2,4,128,256]{3,2,1,0:T(8,128)(2,1)}, bf16[2,4,128,256]{3,2,1,0:T(8,128)(2,1)}, u32[]{:S(2)}, u32[]{:S(2)}) %collective-permute-start.25) | collective-permute-done | bytes 524320 | tf_op jit(solution)/shard_map/ppermute | solution.py:43
  231.2 26.7 %attention.4 = (bf16[512,256]{1,0:T(8,128)(2,1)}, bf16[512,256]{1,0:T(8,128)(2,1)}, bf16[2,4,128,256]{3,2,1,0:T(8,128)(2,1)}, bf16[2,4,128,256]{3,2,1,0:T(8,128)...) custom-call(s32[4,8]{1,0:T(4,128)} %multiply_add_fusion.1.slot_ref, ...), custom_call_target="tpu_custom_call" | custom-call | flops 3221225472 | bytes 8388608 | tf_op jit(solution)/shard_map/attention/pallas_call | solution.py:218
  257.9 5.5 collective-permute-done.35.refs_3_
  268.3 26.6 %attention.5 = (bf16[512,256]{1,0:T(8,128)(2,1)}, bf16[512,256]{1,0:T(8,128)(2,1)}, bf16[2,4,128,256]{3,2,1,0:T(8,128)(2,1)}, bf16[2,4,128,256]{3,2,1,0:T(8,128)...) custom-call(s32[4,8]{1,0:T(4,128)} %get-tuple-element.180.slot_ref, ...), custom_call_target="tpu_custom_call" | custom-call | flops 3221225472 | bytes 8388608 | tf_op jit(solution)/shard_map/attention/pallas_call | solution.py:218
  303.5 26.6 %attention.6 = (bf16[512,256]{1,0:T(8,128)(2,1)}, bf16[512,256]{1,0:T(8,128)(2,1)}, bf16[2,4,128,256]{3,2,1,0:T(8,128)(2,1)}, bf16[2,4,128,256]{3,2,1,0:T(8,128)...) custom-call(s32[4,8]{1,0:T(4,128)} %multiply_add_fusion.1.slot_ref, ...), custom_call_target="tpu_custom_call" | custom-call | flops 3221225472 | bytes 8388608 | tf_op jit(solution)/shard_map/attention/pallas_call | solution.py:218
  337.2 26.6 %attention.7 = (bf16[512,256]{1,0:T(8,128)(2,1)}, bf16[512,256]{1,0:T(8,128)(2,1)}, bf16[2,4,128,256]{3,2,1,0:T(8,128)(2,1)}, bf16[2,4,128,256]{3,2,1,0:T(8,128)...) custom-call(s32[4,8]{1,0:T(4,128)} %get-tuple-element.180.slot_ref, ...), custom_call_target="tpu_custom_call" | custom-call | flops 3221225472 | bytes 8388608 | tf_op jit(solution)/shard_map/attention/pallas_call | solution.py:218
  365.6 4.9 collective-permute-start.61
  370.5 5.4 collective-permute-start.62
  379.5 8.7 %collective-permute-start.65 = (bf16[2,4,128,256]{3,2,1,0:T(8,128)(2,1)}, bf16[2,4,128,256]{3,2,1,0:T(8,128)(2,1)}, u32[]{:S(2)}, u32[]{:S(2)}) collective-permute-start(bf16[2,4,128,256]{3,2,1,0:T(8,128)(2,1)} %get-tuple-element.162), channel_id=1, source_target_pairs={{0,2},{1,3},{2,4},{3,5},{4,6},{5,7},{6,0},{7,1},{8,10},{9,11},{10,... | collective-permute-start | bytes 1572872 | tf_op jit(solution)/shard_map/ppermute | solution.py:43
  392.7 23.9 %collective-permute-start.70 = (bf16[2,4,128,256]{3,2,1,0:T(8,128)(2,1)}, bf16[2,4,128,256]{3,2,1,0:T(8,128)(2,1)S(1)}, u32[]{:S(2)}, u32[]{:S(2)}) collective-permute-start(bf16[2,4,128,256]{3,2,1,0:T(8,128)(2,1)} %get-tuple-element.169), channel_id=1, source_target_pairs={{0,1},{1,0},{2,3},{3,2},{4,5},{5,4},{6,7},{7,6},{8,9},{9,8},{10,11... | collective-permute-start | bytes 1572872 | tf_op jit(solution)/shard_map/ppermute | solution.py:43
  440.0 11.9 %collective-permute-done.72.refs_3_ = bf16[2,4,128,256]{3,2,1,0:T(8,128)(2,1)} collective-permute-done((bf16[2,4,128,256]{3,2,1,0:T(8,128)(2,1)}, bf16[2,4,128,256]{3,2,1,0:T(8,128)(2,1)}, u32[]{:S(2)}, u32[]{:S(2)}) %collective-permute-start.72) | collective-permute-done | bytes 524320 | tf_op jit(solution)/shard_map/ppermute | solution.py:43
  451.9 26.8 %collective-permute-start.48 = (bf16[2,4,128,256]{3,2,1,0:T(8,128)(2,1)}, bf16[2,4,128,256]{3,2,1,0:T(8,128)(2,1)}, u32[]{:S(2)}, u32[]{:S(2)}) collective-permute-start(bf16[2,4,128,256]{3,2,1,0:T(8,128)(2,1)} %get-tuple-element.142), channel_id=1, source_target_pairs={{0,16},{1,17},{2,18},{3,19},{4,20},{5,21},{6,22},{7,23},{8,24},{9,... | collective-permute-start | bytes 1572872 | tf_op jit(solution)/shard_map/ppermute | solution.py:43
  491.3 11.7 %collective-permute-start.67 = (bf16[2,4,128,256]{3,2,1,0:T(8,128)(2,1)}, bf16[2,4,128,256]{3,2,1,0:T(8,128)(2,1)}, u32[]{:S(2)}, u32[]{:S(2)}) collective-permute-start(bf16[2,4,128,256]{3,2,1,0:T(8,128)(2,1)} %get-tuple-element.165), channel_id=1, source_target_pairs={{0,24},{1,25},{2,26},{3,27},{4,28},{5,29},{6,30},{7,31},{8,0},{9,1... | collective-permute-start | bytes 1572872 | tf_op jit(solution)/shard_map/ppermute | solution.py:43
  507.5 4.6 merge.7
  517.9 8.6 %collective-permute-done.67 = bf16[2,4,128,256]{3,2,1,0:T(8,128)(2,1)} collective-permute-done((bf16[2,4,128,256]{3,2,1,0:T(8,128)(2,1)}, bf16[2,4,128,256]{3,2,1,0:T(8,128)(2,1)}, u32[]{:S(2)}, u32[]{:S(2)}) %collective-permute-start.67) | collective-permute-done | bytes 524320 | tf_op jit(solution)/shard_map/ppermute | solution.py:43
  528.2 10.9 %collective-permute-done.69 = bf16[2,4,128,256]{3,2,1,0:T(8,128)(2,1)S(1)} collective-permute-done((bf16[2,4,128,256]{3,2,1,0:T(8,128)(2,1)}, bf16[2,4,128,256]{3,2,1,0:T(8,128)(2,1)S(1)}, u32[]{:S(2)}, u32[]{:S(2)}) %collective-permute-start.69) | collective-permute-done | bytes 524320 | tf_op jit(solution)/shard_map/ppermute | solution.py:43
  (304 shorter events, 184.8 us)
Async XLA Ops:
  67.8 48.9 %collective-permute-start.5 = (bf16[2,4,128,256]{3,2,1,0:T(8,128)(2,1)}, bf16[2,4,128,256]{3,2,1,0:T(8,128)(2,1)}, u32[]{:S(2)}, u32[]{:S(2)}) collective-permute-start(bf16[2,4,128,256]{3,2,1,0:T(8,128)(2,1)} %get-tuple-element.95), channel_id=1, source_target_pairs={{0,3},{1,2},{2,5},{3,4},{4,7},{5,6},{6,1},{7,0},{8,11},{9,10},{10,... | collective-permute-start | bytes 1572872 | tf_op jit(solution)/shard_map/ppermute | solution.py:43
  72.8 473.5 %reduce-scatter.2.cloned.1.call-start = ((), (), s32[]{:S(2)}) async-start(), calls=%async_computation.3 | async-start | bytes 2162688 | tf_op jit(solution)/shard_map/reduce_scatter | solution.py:315
  89.6 43.2 %collective-permute-start.9 = (bf16[2,4,128,256]{3,2,1,0:T(8,128)(2,1)}, bf16[2,4,128,256]{3,2,1,0:T(8,128)(2,1)S(1)}, u32[]{:S(2)}, u32[]{:S(2)}) collective-permute-start(bf16[2,4,128,256]{3,2,1,0:T(8,128)(2,1)} %get-tuple-element.99), channel_id=1, source_target_pairs={{0,7},{1,6},{2,1},{3,0},{4,3},{5,2},{6,5},{7,4},{8,15},{9,14},{10,... | collective-permute-start | bytes 1572872 | tf_op jit(solution)/shard_map/ppermute | solution.py:43
  116.8 48.9 %collective-permute-start.15 = (bf16[2,4,128,256]{3,2,1,0:T(8,128)(2,1)}, bf16[2,4,128,256]{3,2,1,0:T(8,128)(2,1)}, u32[]{:S(2)}, u32[]{:S(2)}) collective-permute-start(bf16[2,4,128,256]{3,2,1,0:T(8,128)(2,1)} %get-tuple-element.104), channel_id=1, source_target_pairs={{0,9},{1,8},{2,11},{3,10},{4,13},{5,12},{6,15},{7,14},{8,17},{9,16... | collective-permute-start | bytes 1572872 | tf_op jit(solution)/shard_map/ppermute | solution.py:43
  120.4 45.3 %collective-permute-start.16 = (bf16[2,4,128,256]{3,2,1,0:T(8,128)(2,1)}, bf16[2,4,128,256]{3,2,1,0:T(8,128)(2,1)}, u32[]{:S(2)}, u32[]{:S(2)}) collective-permute-start(bf16[2,4,128,256]{3,2,1,0:T(8,128)(2,1)} %get-tuple-element.105), channel_id=1, source_target_pairs={{0,16},{1,17},{2,18},{3,19},{4,20},{5,21},{6,22},{7,23},{8,24},{9,... | collective-permute-start | bytes 1572872 | tf_op jit(solution)/shard_map/ppermute | solution.py:43
  165.8 48.9 %collective-permute-start.25 = (bf16[2,4,128,256]{3,2,1,0:T(8,128)(2,1)}, bf16[2,4,128,256]{3,2,1,0:T(8,128)(2,1)}, u32[]{:S(2)}, u32[]{:S(2)}) collective-permute-start(bf16[2,4,128,256]{3,2,1,0:T(8,128)(2,1)} %get-tuple-element.113), channel_id=1, source_target_pairs={{0,3},{1,2},{2,5},{3,4},{4,7},{5,6},{6,1},{7,0},{8,11},{9,10},{10,... | collective-permute-start | bytes 1572872 | tf_op jit(solution)/shard_map/ppermute | solution.py:43
  165.9 48.8 %collective-permute-start.26 = (bf16[2,4,128,256]{3,2,1,0:T(8,128)(2,1)}, bf16[2,4,128,256]{3,2,1,0:T(8,128)(2,1)}, u32[]{:S(2)}, u32[]{:S(2)}) collective-permute-start(bf16[2,4,128,256]{3,2,1,0:T(8,128)(2,1)} %get-tuple-element.114), channel_id=1, source_target_pairs={{0,4},{1,5},{2,6},{3,7},{4,0},{5,1},{6,2},{7,3},{8,12},{9,13},{10,... | collective-permute-start | bytes 1572872 | tf_op jit(solution)/shard_map/ppermute | solution.py:43
  175.0 43.1 %collective-permute-start.27 = (bf16[2,4,128,256]{3,2,1,0:T(8,128)(2,1)}, bf16[2,4,128,256]{3,2,1,0:T(8,128)(2,1)S(1)}, u32[]{:S(2)}, u32[]{:S(2)}) collective-permute-start(bf16[2,4,128,256]{3,2,1,0:T(8,128)(2,1)} %get-tuple-element.115), channel_id=1, source_target_pairs={{0,5},{1,4},{2,7},{3,6},{4,1},{5,0},{6,3},{7,2},{8,13},{9,12},{10,... | collective-permute-start | bytes 1572872 | tf_op jit(solution)/shard_map/ppermute | solution.py:43
  175.2 43.1 %collective-permute-start.28 = (bf16[2,4,128,256]{3,2,1,0:T(8,128)(2,1)}, bf16[2,4,128,256]{3,2,1,0:T(8,128)(2,1)S(1)}, u32[]{:S(2)}, u32[]{:S(2)}) collective-permute-start(bf16[2,4,128,256]{3,2,1,0:T(8,128)(2,1)} %get-tuple-element.116), channel_id=1, source_target_pairs={{0,6},{1,7},{2,0},{3,1},{4,2},{5,3},{6,4},{7,5},{8,14},{9,15},{10,... | collective-permute-start | bytes 1572872 | tf_op jit(solution)/shard_map/ppermute | solution.py:43
  180.3 42.4 %collective-permute-start.29 = (bf16[2,4,128,256]{3,2,1,0:T(8,128)(2,1)}, bf16[2,4,128,256]{3,2,1,0:T(8,128)(2,1)S(1)}, u32[]{:S(2)}, u32[]{:S(2)}) collective-permute-start(bf16[2,4,128,256]{3,2,1,0:T(8,128)(2,1)} %get-tuple-element.117), channel_id=1, source_target_pairs={{0,7},{1,6},{2,1},{3,0},{4,3},{5,2},{6,5},{7,4},{8,15},{9,14},{10,... | collective-permute-start | bytes 1572872 | tf_op jit(solution)/shard_map/ppermute | solution.py:43
  218.2 45.3 %collective-permute-start.35 = (bf16[2,4,128,256]{3,2,1,0:T(8,128)(2,1)}, bf16[2,4,128,256]{3,2,1,0:T(8,128)(2,1)S(1)}, u32[]{:S(2)}, u32[]{:S(2)}) collective-permute-start(bf16[2,4,128,256]{3,2,1,0:T(8,128)(2,1)} %get-tuple-element.122), channel_id=1, source_target_pairs={{0,9},{1,8},{2,11},{3,10},{4,13},{5,12},{6,15},{7,14},{8,17},{9,16... | collective-permute-start | bytes 1572872 | tf_op jit(solution)/shard_map/ppermute | solution.py:43
  218.3 45.2 %collective-permute-start.36 = (bf16[2,4,128,256]{3,2,1,0:T(8,128)(2,1)}, bf16[2,4,128,256]{3,2,1,0:T(8,128)(2,1)S(1)}, u32[]{:S(2)}, u32[]{:S(2)}) collective-permute-start(bf16[2,4,128,256]{3,2,1,0:T(8,128)(2,1)} %get-tuple-element.123), channel_id=1, source_target_pairs={{0,16},{1,17},{2,18},{3,19},{4,20},{5,21},{6,22},{7,23},{8,24},{9,... | collective-permute-start | bytes 1572872 | tf_op jit(solution)/shard_map/ppermute | solution.py:43
  222.8 40.9 %collective-permute-start.37 = (bf16[2,4,128,256]{3,2,1,0:T(8,128)(2,1)}, bf16[2,4,128,256]{3,2,1,0:T(8,128)(2,1)S(1)}, u32[]{:S(2)}, u32[]{:S(2)}) collective-permute-start(bf16[2,4,128,256]{3,2,1,0:T(8,128)(2,1)} %get-tuple-element.124), channel_id=1, source_target_pairs={{0,17},{1,16},{2,19},{3,18},{4,21},{5,20},{6,23},{7,22},{8,25},{9,... | collective-permute-start | bytes 1572872 | tf_op jit(solution)/shard_map/ppermute | solution.py:43
  222.8 41.2 %collective-permute-start.38 = (bf16[2,4,128,256]{3,2,1,0:T(8,128)(2,1)}, bf16[2,4,128,256]{3,2,1,0:T(8,128)(2,1)S(1)}, u32[]{:S(2)}, u32[]{:S(2)}) collective-permute-start(bf16[2,4,128,256]{3,2,1,0:T(8,128)(2,1)} %get-tuple-element.125), channel_id=1, source_target_pairs={{0,24},{1,25},{2,26},{3,27},{4,28},{5,29},{6,30},{7,31},{8,0},{9,1... | collective-permute-start | bytes 1572872 | tf_op jit(solution)/shard_map/ppermute | solution.py:43
  330.6 39.9 %collective-permute-start.54 = (bf16[2,4,128,256]{3,2,1,0:T(8,128)(2,1)}, bf16[2,4,128,256]{3,2,1,0:T(8,128)(2,1)S(1)}, u32[]{:S(2)}, u32[]{:S(2)}) collective-permute-start(bf16[2,4,128,256]{3,2,1,0:T(8,128)(2,1)} %get-tuple-element.149), channel_id=1, source_target_pairs={{0,17},{1,16},{2,19},{3,18},{4,21},{5,20},{6,23},{7,22},{8,25},{9,... | collective-permute-start | bytes 1572872 | tf_op jit(solution)/shard_map/ppermute | solution.py:43
  333.7 42.2 %collective-permute-start.55 = (bf16[2,4,128,256]{3,2,1,0:T(8,128)(2,1)}, bf16[2,4,128,256]{3,2,1,0:T(8,128)(2,1)S(1)}, u32[]{:S(2)}, u32[]{:S(2)}) collective-permute-start(bf16[2,4,128,256]{3,2,1,0:T(8,128)(2,1)} %get-tuple-element.150), channel_id=1, source_target_pairs={{0,8},{1,9},{2,10},{3,11},{4,12},{5,13},{6,14},{7,15},{8,16},{9,17... | collective-permute-start | bytes 1572872 | tf_op jit(solution)/shard_map/ppermute | solution.py:43
  333.7 45.8 %collective-permute-start.56 = (bf16[2,4,128,256]{3,2,1,0:T(8,128)(2,1)}, bf16[2,4,128,256]{3,2,1,0:T(8,128)(2,1)S(1)}, u32[]{:S(2)}, u32[]{:S(2)}) collective-permute-start(bf16[2,4,128,256]{3,2,1,0:T(8,128)(2,1)} %get-tuple-element.151), channel_id=1, source_target_pairs={{0,9},{1,8},{2,11},{3,10},{4,13},{5,12},{6,15},{7,14},{8,17},{9,16... | collective-permute-start | bytes 1572872 | tf_op jit(solution)/shard_map/ppermute | solution.py:43
  335.2 44.4 %collective-permute-start.60 = (bf16[2,4,128,256]{3,2,1,0:T(8,128)(2,1)}, bf16[2,4,128,256]{3,2,1,0:T(8,128)(2,1)S(1)}, u32[]{:S(2)}, u32[]{:S(2)}) collective-permute-start(bf16[2,4,128,256]{3,2,1,0:T(8,128)(2,1)} %get-tuple-element.157), channel_id=1, source_target_pairs={{0,1},{1,0},{2,3},{3,2},{4,5},{5,4},{6,7},{7,6},{8,9},{9,8},{10,11... | collective-permute-start | bytes 1572872 | tf_op jit(solution)/shard_map/ppermute | solution.py:43
  375.9 40.7 %collective-permute-start.63 = (bf16[2,4,128,256]{3,2,1,0:T(8,128)(2,1)}, bf16[2,4,128,256]{3,2,1,0:T(8,128)(2,1)}, u32[]{:S(2)}, u32[]{:S(2)}) collective-permute-start(bf16[2,4,128,256]{3,2,1,0:T(8,128)(2,1)} %get-tuple-element.160), channel_id=1, source_target_pairs={{0,4},{1,5},{2,6},{3,7},{4,0},{5,1},{6,2},{7,3},{8,12},{9,13},{10,... | collective-permute-start | bytes 1572872 | tf_op jit(solution)/shard_map/ppermute | solution.py:43
  379.5 40.0 %collective-permute-start.64 = (bf16[2,4,128,256]{3,2,1,0:T(8,128)(2,1)}, bf16[2,4,128,256]{3,2,1,0:T(8,128)(2,1)}, u32[]{:S(2)}, u32[]{:S(2)}) collective-permute-start(bf16[2,4,128,256]{3,2,1,0:T(8,128)(2,1)} %get-tuple-element.161), channel_id=1, source_target_pairs={{0,5},{1,4},{2,7},{3,6},{4,1},{5,0},{6,3},{7,2},{8,13},{9,12},{10,... | collective-permute-start | bytes 1572872 | tf_op jit(solution)/shard_map/ppermute | solution.py:43
  379.5 44.3 %collective-permute-start.65 = (bf16[2,4,128,256]{3,2,1,0:T(8,128)(2,1)}, bf16[2,4,128,256]{3,2,1,0:T(8,128)(2,1)}, u32[]{:S(2)}, u32[]{:S(2)}) collective-permute-start(bf16[2,4,128,256]{3,2,1,0:T(8,128)(2,1)} %get-tuple-element.162), channel_id=1, source_target_pairs={{0,2},{1,3},{2,4},{3,5},{4,6},{5,7},{6,0},{7,1},{8,10},{9,11},{10,... | collective-permute-start | bytes 1572872 | tf_op jit(solution)/shard_map/ppermute | solution.py:43
  426.7 56.5 %collective-permute-start.74 = (bf16[2,4,128,256]{3,2,1,0:T(8,128)(2,1)}, bf16[2,4,128,256]{3,2,1,0:T(8,128)(2,1)}, u32[]{:S(2)}, u32[]{:S(2)}) collective-permute-start(bf16[2,4,128,256]{3,2,1,0:T(8,128)(2,1)} %get-tuple-element.173), channel_id=1, source_target_pairs={{0,17},{1,16},{2,19},{3,18},{4,21},{5,20},{6,23},{7,22},{8,25},{9,... | collective-permute-start | bytes 1572872 | tf_op jit(solution)/shard_map/ppermute | solution.py:43
  428.8 54.6 %collective-permute-start.75 = (bf16[2,4,128,256]{3,2,1,0:T(8,128)(2,1)}, bf16[2,4,128,256]{3,2,1,0:T(8,128)(2,1)}, u32[]{:S(2)}, u32[]{:S(2)}) collective-permute-start(bf16[2,4,128,256]{3,2,1,0:T(8,128)(2,1)} %get-tuple-element.174), channel_id=1, source_target_pairs={{0,8},{1,9},{2,10},{3,11},{4,12},{5,13},{6,14},{7,15},{8,16},{9,17... | collective-permute-start | bytes 1572872 | tf_op jit(solution)/shard_map/ppermute | solution.py:43
  437.5 52.3 %collective-permute-start.76 = (bf16[2,4,128,256]{3,2,1,0:T(8,128)(2,1)}, bf16[2,4,128,256]{3,2,1,0:T(8,128)(2,1)}, u32[]{:S(2)}, u32[]{:S(2)}) collective-permute-start(bf16[2,4,128,256]{3,2,1,0:T(8,128)(2,1)} %get-tuple-element.175), channel_id=1, source_target_pairs={{0,9},{1,8},{2,11},{3,10},{4,13},{5,12},{6,15},{7,14},{8,17},{9,16... | collective-permute-start | bytes 1572872 | tf_op jit(solution)/shard_map/ppermute | solution.py:43
  (116 other events, 3151.9 us)
Sparse Core Ops, SparseCore 0:
  392.5 122.6 reduce-scatter.1

commit v2 on v1

--- a/solution.py
+++ b/solution.py
@@ -22,9 +22,6 @@
 DESTS = 8
 masked_score = -1e30
 ROWS = [[y * NZ * NCORE + i for i in range(NZ * NCORE)] for y in range(NY)]
-COLUMNS = [
-    [(y * NZ + z) * NCORE + c for y in range(NY) for c in range(NCORE)] for z in range(NZ)
-]
 
 
 def shift(dy, dz, dc):
@@ -112,92 +109,77 @@
     tiles = refs[:8]
     o_ref, dq_ref = refs[8:10]
     grads = refs[10:18]
-    keys, values, d_keys, d_values, query2, d_out2, scores, sums = refs[18:]
+    keys, values, d_keys, d_values, own_keys, own_values, scores, weights, d_scores = refs[18:]
+    entries = slot_ref.shape[1]
     for d in range(DESTS):
         for k in range(4):
             keys[4 * d + k] = tiles[d][0, k]
             values[4 * d + k] = tiles[d][1, k]
     d_keys[...] = jnp.zeros_like(d_keys)
     d_values[...] = jnp.zeros_like(d_values)
-    first = lax.broadcasted_iota(jnp.int32, (EB, PAIR), 1) < HEAD_DIM
-    zero = jnp.zeros((EB, PAIR), jnp.bfloat16)
-    trips = count_ref[0]
-    for b in range(blocks):
-        rows = slice(b * EB, (b + 1) * EB)
+
+    def split(x, axis):
+        low = lax.broadcasted_iota(jnp.int32, x.shape, 1 - axis) < HEAD_DIM
+        zero = jnp.zeros_like(x)
+        return jnp.concatenate([jnp.where(low, x, zero), jnp.where(low, zero, x)], axis=axis)
+
+    def join(x):
+        return jnp.concatenate([x[:HEAD_DIM, :EB], x[HEAD_DIM:, EB:]], axis=0)
+
+    def fold(x, op):
+        return op(x.reshape(TILE // 8, 8, 2 * EB), axis=0)
+
+    def block_step(b, carry):
+        rows = pl.ds(pl.multiple_of(b * EB, EB), EB)
+        count = count_ref[b]
         query = q_ref[rows, :] * jnp.bfloat16(SCALE)
-        query2[b, :EB, :] = jnp.where(first, query, zero)
-        query2[b, EB:, :] = jnp.where(first, zero, query)
-        d_out = do_ref[rows, :]
-        d_out2[b, :EB, :] = jnp.where(first, d_out, zero)
-        d_out2[b, EB:, :] = jnp.where(first, zero, d_out)
-        trips = jnp.maximum(trips, count_ref[b])
-
-    def score_step(j, maxima):
-        updated = []
-        for b in range(blocks):
-            logits = dot(keys[slot_ref[b, j]], query2[b], 1, 1)
-            logits = jnp.where(j < count_ref[b], logits, masked_score)
-            scores[b, j] = logits
-            updated.append(
-                jnp.maximum(maxima[b], jnp.max(logits.reshape(TILE // 8, 8, 2 * EB), axis=0))
-            )
-        return tuple(updated)
-
-    maxima = lax.fori_loop(
-        0, trips, score_step, (jnp.full((8, 2 * EB), masked_score, jnp.float32),) * blocks
-    )
-    row_max = [jnp.max(m, axis=0, keepdims=True) for m in maxima]
-    sums[...] = jnp.zeros_like(sums)
-
-    def output_step(j, totals):
-        updated = []
-        for b in range(blocks):
-            weight = jnp.exp(scores[b, j] - row_max[b])
-            scores[b, j] = weight
-            updated.append(totals[b] + jnp.sum(weight.reshape(TILE // 8, 8, 2 * EB), axis=0))
-            sums[b] += dot(values[slot_ref[b, j]], weight.astype(jnp.bfloat16), 0, 0)
-        return tuple(updated)
-
-    totals = lax.fori_loop(
-        0, trips, output_step, (jnp.zeros((8, 2 * EB), jnp.float32),) * blocks
-    )
-    inverse = [1.0 / jnp.sum(t, axis=0, keepdims=True) for t in totals]
-    delta = []
-    for b in range(blocks):
-        rows = slice(b * EB, (b + 1) * EB)
-        out2 = sums[b] * inverse[b]
-        out = jnp.concatenate([out2[:HEAD_DIM, :EB], out2[HEAD_DIM:, EB:]], axis=0)
-        product = out * do_ref[rows, :].astype(jnp.float32).T
-        delta.append(
-            jnp.concatenate(
-                [
-                    jnp.sum(product[:HEAD_DIM], axis=0, keepdims=True),
-                    jnp.sum(product[HEAD_DIM:], axis=0, keepdims=True),
-                ],
-                axis=1,
-            )
+        query2 = split(query, 0)
+        parts = [slice(j * TILE, (j + 1) * TILE) for j in range(entries)]
+        for j in range(entries):
+            own_keys[parts[j], :] = keys[slot_ref[b, j]]
+            own_values[parts[j], :] = values[slot_ref[b, j]]
+        logits = dot(own_keys[...], query2, 1, 1)
+        maxima = jnp.full((8, 2 * EB), masked_score, jnp.float32)
+        for j in range(entries):
+            masked = jnp.where(j < count, logits[parts[j]], masked_score)
+            scores[parts[j], :] = masked
+            maxima = jnp.maximum(maxima, fold(masked, jnp.max))
+        row_max = jnp.max(maxima, axis=0, keepdims=True)
+        total = jnp.zeros((8, 2 * EB), jnp.float32)
+        for j in range(entries):
+            weight = jnp.exp(scores[parts[j], :] - row_max)
+            total += fold(weight, jnp.sum)
+            weights[parts[j], :] = weight.astype(jnp.bfloat16)
+        inverse = 1.0 / jnp.sum(total, axis=0, keepdims=True)
+        out = join(dot(own_values[...], weights[...], 0, 0) * inverse)
+        d_out = do_ref[rows, :].astype(jnp.float32).T
+        product = out * d_out
+        delta = jnp.concatenate(
+            [
+                jnp.sum(product[:HEAD_DIM], axis=0, keepdims=True),
+                jnp.sum(product[HEAD_DIM:], axis=0, keepdims=True),
+            ],
+            axis=1,
         )
+        delta = delta * inverse
         o_ref[rows, :] = out.T.astype(jnp.bfloat16)
-    sums[...] = jnp.zeros_like(sums)
-
-    def grad_step(j, carry):
-        for b in range(blocks):
-            slot = slot_ref[b, j]
-            weight = scores[b, j] * inverse[b]
-            d_weight = dot(values[slot], d_out2[b], 1, 1)
-            d_score = (weight * (d_weight - delta[b])).astype(jnp.bfloat16)
-            d_values[slot] += dot(weight.astype(jnp.bfloat16), d_out2[b], 1, 0)
-            d_keys[slot] += dot(d_score, query2[b], 1, 0)
-            sums[b] += dot(keys[slot], d_score, 0, 0)
+        low = lax.broadcasted_iota(jnp.int32, (PAIR, EB), 0) < HEAD_DIM
+        scaled = d_out * jnp.where(low, inverse[:, :EB], inverse[:, EB:])
+        d_out2 = split(scaled.T.astype(jnp.bfloat16), 0)
+        d_weights = dot(own_values[...], d_out2, 1, 1)
+        for j in range(entries):
+            change = (d_weights[parts[j]] - delta).astype(jnp.bfloat16)
+            d_scores[parts[j], :] = weights[parts[j], :] * change
+        value_terms = dot(weights[...], d_out2, 1, 0)
+        key_terms = dot(d_scores[...], query2, 1, 0)
+        for j in range(entries):
+            d_values[slot_ref[b, j]] += value_terms[parts[j]]
+            d_keys[slot_ref[b, j]] += key_terms[parts[j]]
+        d_query = join(dot(own_keys[...], d_scores[...], 0, 0))
+        dq_ref[rows, :] = (d_query.T * SCALE).astype(jnp.bfloat16)
         return carry
 
-    lax.fori_loop(0, trips, grad_step, 0)
-    for b in range(blocks):
-        d_query2 = sums[b]
-        d_query = jnp.concatenate(
-            [d_query2[:HEAD_DIM, :EB], d_query2[HEAD_DIM:, EB:]], axis=0
-        )
-        dq_ref[b * EB : (b + 1) * EB, :] = (d_query.T * SCALE).astype(jnp.bfloat16)
+    lax.fori_loop(0, blocks, block_step, 0, unroll=2)
     for d in range(DESTS):
         for k in range(4):
             grads[d][0, k] = d_keys[4 * d + k].astype(jnp.bfloat16)
@@ -227,10 +209,11 @@
                 pltpu.VMEM((work, TILE, PAIR), jnp.bfloat16),
                 pltpu.VMEM((work, TILE, PAIR), jnp.float32),
                 pltpu.VMEM((work, TILE, PAIR), jnp.float32),
-                pltpu.VMEM((blocks, 2 * EB, PAIR), jnp.bfloat16),
-                pltpu.VMEM((blocks, 2 * EB, PAIR), jnp.bfloat16),
-                pltpu.VMEM((blocks, entries, TILE, 2 * EB), jnp.float32),
-                pltpu.VMEM((blocks, PAIR, 2 * EB), jnp.float32),
+                pltpu.VMEM((entries * TILE, PAIR), jnp.bfloat16),
+                pltpu.VMEM((entries * TILE, PAIR), jnp.bfloat16),
+                pltpu.VMEM((entries * TILE, 2 * EB), jnp.float32),
+                pltpu.VMEM((entries * TILE, 2 * EB), jnp.bfloat16),
+                pltpu.VMEM((entries * TILE, 2 * EB), jnp.bfloat16),
             ],
         ),
         out_shape=[out, out] + [grad] * DESTS,
@@ -255,15 +238,16 @@
     usable = jnp.arange(tile_ids.shape[1])[None, :] < tile_count[:, None]
     matches = (source[:, :, None] == jnp.arange(devices)[None, None, :]) & usable[:, :, None]
     wanted = jnp.max(jnp.where(matches, within[:, :, None], -1), axis=(0, 1))
-    told = [
-        lax.all_to_all(
-            operand, "seq", 0, 0, axis_index_groups=groups, tiled=True
-        ).reshape(-1, NCORE, 4)
-        for operand, groups in (
-            (wanted.reshape(NY, NZ * NCORE).T, ROWS),
-            (wanted.reshape(NY, NZ, NCORE).transpose(0, 2, 1).reshape(-1, NZ), COLUMNS),
-        )
-    ]
+    grid = wanted.reshape(NY, NZ, NCORE)
+    along = jnp.concatenate(
+        [
+            jnp.broadcast_to(grid.transpose(1, 2, 0)[None], (NY, NZ, NCORE, NY)),
+            jnp.broadcast_to(grid.transpose(0, 2, 1)[:, None], (NY, NZ, NCORE, NZ)),
+        ],
+        axis=3,
+    )
+    told = lax.all_to_all(along.reshape(devices, NY + NZ), "seq", 0, 0, tiled=True)
+    told = told.reshape(NY, NZ, NCORE, NY + NZ)
     source_y, source_z = source // (NZ * NCORE), (source // NCORE) % NZ
     flip = (source % NCORE) ^ c
     back_y, back_z = (y - source_y) % NY, (z - source_z) % NZ
@@ -275,15 +259,15 @@
     core = c ^ jnp.arange(NCORE)[None, :, None]
     near = jnp.arange(4)[None, None, :]
     asked = (
-        told[0][(z + far) % NZ, core, (y - near) % NY].reshape(DESTS, 4),
-        told[1][(y + far) % NY, core, (z - near) % NZ].reshape(DESTS, 4),
+        told[y, (z + far) % NZ, core, (y - near) % NY].reshape(DESTS, 4),
+        told[(y + far) % NY, z, core, NY + (z - near) % NZ].reshape(DESTS, 4),
     )
 
     d_attended = lax.dot_general(
         out_grad, out_weight, (((1,), (1,)), ((), ())), preferred_element_type=jnp.float32
     ).astype(jnp.bfloat16)
 
-    attended, d_queries, d_kv = [], [], []
+    attended, d_queries, d_kv, partials = [], [], [], []
     for chunk in range(CHUNKS):
         along_y = chunk % 2 == 0
         kind = 0 if along_y else 1
@@ -300,6 +284,16 @@
         packed = pack(jnp.maximum(asked[kind], 0), held)
         tiles = [far_move(packed[d], d, 1) for d in range(DESTS)]
         out, d_query, grads = attention(chunk, slots[kind], tile_count, queries, d_attended, tiles)
+        product = dot(out, out_grad, 0, 0).astype(jnp.bfloat16)
+        partials.append(
+            lax.psum_scatter(
+                product,
+                "seq",
+                scatter_dimension=0,
+                axis_index_groups=ROWS,
+                tiled=True,
+            )
+        )
         attended.append(out)
         d_queries.append(d_query)
         parts = [far_move(grads[d], d, -1) for d in range(DESTS)]
@@ -309,12 +303,12 @@
         d_kv.append(total.astype(jnp.bfloat16))
     attended = jnp.concatenate(attended, axis=1)
     joined = jnp.dot(attended, out_weight, preferred_element_type=jnp.float32).astype(jnp.bfloat16)
-    product = lax.dot_general(
-        attended, out_grad, (((0,), (0,)), ((), ())), preferred_element_type=jnp.float32
-    ).astype(jnp.bfloat16)
-    d_out_weight = lax.psum_scatter(
-        product, "seq", scatter_dimension=0, tiled=True
-    ).astype(jnp.float32)
+    partials = jnp.stack(partials)
+    arrived = [
+        move(lax.dynamic_index_in_dim(partials, (y - k) % NY, 0, keepdims=False), -k, 0, 0)
+        for k in range(NY)
+    ]
+    d_out_weight = sum(part.astype(jnp.float32) for part in arrived)
     d_queries = jnp.concatenate(d_queries, axis=1)
     d_kv = jnp.concatenate(d_kv, axis=3).reshape(rgb_kv.shape)
     return (joined, d_queries, d_kv, d_out_weight)

time: 565 us -> 581 us (1.028)
  the two profiles are of different devices: /device:TPU:7 before, /device:TPU:1 now
where the time goes in v2:
time: 581 us; the launch traced here: 572 us
  waiting for transfers between devices  277 us (48%)
  starting transfers between devices  150 us (26%)
  Pallas kernels  97.4 us (17%)
  between operations  14.5 us (2%)
  matrix products  14.4 us (2%)
  other arithmetic  13.8 us (2%)
    ppermute x83, waiting for transfers between devices, move(): return lax.ppermute(x, 'seq', shift(dy, dz, dc))  277 us
    ppermute x83, starting transfers between devices, move(): return lax.ppermute(x, 'seq', shift(dy, dz, dc))  141 us
    pallas_call x4, Pallas kernels, attention(): pl.pallas_call(functools.partial(attention_kernel, blocks), grid_spec=plt...  61.2 us
    pallas_call x4, Pallas kernels, merge(): pl.pallas_call(merge_kernel, grid_spec=pltpu.PrefetchScalarGridSpec(num_s...  18.1 us
    pallas_call x4, Pallas kernels, pack(): pl.pallas_call(pack_kernel, grid_spec=pltpu.PrefetchScalarGridSpec(num_sc...  18 us
  transfers between devices with their start and end apart: 88, of which 30 were waited for; matrix products, arithmetic and copies ran while one was open for 5% of the time, Pallas kernels for 17%

profile of v2, /device:TPU:1, one launch (start us, length us, event | category | flops | bytes accessed | tf_op | source)
XLA Modules:
  0.0 572.0 jit_solution(6951863395497637025)
XLA Ops:
  20.2 8.5 %all-to-all-start = ((s32[32,1,8]{2,1,0:T(1,128)}), s32[32,1,8]{2,1,0:T(1,128)S(1)}, u32[]{:S(2)}, u32[]{:S(2)}) async-start(s32[32,1,8]{2,1,0:T(1,128)} %bitcast.2), calls=%async_computation | async-start | bytes 32768 | tf_op jit(solution)/shard_map/all_to_all | solution.py:249
  47.2 26.0 %collective-permute-done.10.refs_1_ = bf16[2,4,128,256]{3,2,1,0:T(8,128)(2,1)} collective-permute-done((bf16[2,4,128,256]{3,2,1,0:T(8,128)(2,1)}, bf16[2,4,128,256]{3,2,1,0:T(8,128)(2,1)}, u32[]{:S(2)}, u32[]{:S(2)}) %collective-permute-start.10) | collective-permute-done | bytes 524320 | tf_op jit(solution)/shard_map/ppermute | solution.py:40
  112.8 10.5 %collective-permute-done.15.refs_3_ = bf16[2,4,128,256]{3,2,1,0:T(8,128)(2,1)} collective-permute-done((bf16[2,4,128,256]{3,2,1,0:T(8,128)(2,1)}, bf16[2,4,128,256]{3,2,1,0:T(8,128)(2,1)}, u32[]{:S(2)}, u32[]{:S(2)}) %collective-permute-start.15) | collective-permute-done | bytes 524320 | tf_op jit(solution)/shard_map/ppermute | solution.py:40
  123.7 8.9 %collective-permute-done.16.refs_4_ = bf16[2,4,128,256]{3,2,1,0:T(8,128)(2,1)S(1)} collective-permute-done((bf16[2,4,128,256]{3,2,1,0:T(8,128)(2,1)}, bf16[2,4,128,256]{3,2,1,0:T(8,128)(2,1)S(1)}, u32[]{:S(2)}, u32[]{:S(2)}) %collective-permute-start.16) | collective-permute-done | bytes 524320 | tf_op jit(solution)/shard_map/ppermute | solution.py:40
  132.5 13.0 %collective-permute-done.17.refs_5_ = bf16[2,4,128,256]{3,2,1,0:T(8,128)(2,1)S(1)} collective-permute-done((bf16[2,4,128,256]{3,2,1,0:T(8,128)(2,1)}, bf16[2,4,128,256]{3,2,1,0:T(8,128)(2,1)S(1)}, u32[]{:S(2)}, u32[]{:S(2)}) %collective-permute-start.17) | collective-permute-done | bytes 524320 | tf_op jit(solution)/shard_map/ppermute | solution.py:40
  158.0 10.2 %collective-permute-done.35.refs_3_ = bf16[2,4,128,256]{3,2,1,0:T(8,128)(2,1)} collective-permute-done((bf16[2,4,128,256]{3,2,1,0:T(8,128)(2,1)}, bf16[2,4,128,256]{3,2,1,0:T(8,128)(2,1)}, u32[]{:S(2)}, u32[]{:S(2)}) %collective-permute-start.35) | collective-permute-done | bytes 524320 | tf_op jit(solution)/shard_map/ppermute | solution.py:40
  168.5 9.1 %collective-permute-done.36.refs_4_ = bf16[2,4,128,256]{3,2,1,0:T(8,128)(2,1)} collective-permute-done((bf16[2,4,128,256]{3,2,1,0:T(8,128)(2,1)}, bf16[2,4,128,256]{3,2,1,0:T(8,128)(2,1)}, u32[]{:S(2)}, u32[]{:S(2)}) %collective-permute-start.36) | collective-permute-done | bytes 524320 | tf_op jit(solution)/shard_map/ppermute | solution.py:40
  177.6 12.0 %collective-permute-done.37.refs_5_ = bf16[2,4,128,256]{3,2,1,0:T(8,128)(2,1)} collective-permute-done((bf16[2,4,128,256]{3,2,1,0:T(8,128)(2,1)}, bf16[2,4,128,256]{3,2,1,0:T(8,128)(2,1)}, u32[]{:S(2)}, u32[]{:S(2)}) %collective-permute-start.37) | collective-permute-done | bytes 524320 | tf_op jit(solution)/shard_map/ppermute | solution.py:40
  202.8 24.1 %collective-permute-done.25.refs_3_ = bf16[2,4,128,256]{3,2,1,0:T(8,128)(2,1)} collective-permute-done((bf16[2,4,128,256]{3,2,1,0:T(8,128)(2,1)}, bf16[2,4,128,256]{3,2,1,0:T(8,128)(2,1)}, u32[]{:S(2)}, u32[]{:S(2)}) %collective-permute-start.25) | collective-permute-done | bytes 524320 | tf_op jit(solution)/shard_map/ppermute | solution.py:40
  227.5 15.5 %attention.5 = (bf16[512,256]{1,0:T(8,128)(2,1)}, bf16[512,256]{1,0:T(8,128)(2,1)}, bf16[2,4,128,256]{3,2,1,0:T(8,128)(2,1)}, bf16[2,4,128,256]{3,2,1,0:T(8,128)...) custom-call(s32[4,8]{1,0:T(4,128)} %multiply_add_fusion.slot_ref, ...), custom_call_target="tpu_custom_call" | custom-call | flops 3221225472 | bytes 8388608 | tf_op jit(solution)/shard_map/attention/pallas_call | solution.py:200
  258.8 13.7 %collective-permute-done.6.refs_4_ = bf16[2,4,128,256]{3,2,1,0:T(8,128)(2,1)} collective-permute-done((bf16[2,4,128,256]{3,2,1,0:T(8,128)(2,1)}, bf16[2,4,128,256]{3,2,1,0:T(8,128)(2,1)}, u32[]{:S(2)}, u32[]{:S(2)}) %collective-permute-start.6) | collective-permute-done | bytes 524320 | tf_op jit(solution)/shard_map/ppermute | solution.py:40
  272.5 11.5 %collective-permute-done.7.refs_5_ = bf16[2,4,128,256]{3,2,1,0:T(8,128)(2,1)} collective-permute-done((bf16[2,4,128,256]{3,2,1,0:T(8,128)(2,1)}, bf16[2,4,128,256]{3,2,1,0:T(8,128)(2,1)}, u32[]{:S(2)}, u32[]{:S(2)}) %collective-permute-start.7) | collective-permute-done | bytes 524320 | tf_op jit(solution)/shard_map/ppermute | solution.py:40
  284.9 10.8 %collective-permute-done.9.refs_7_ = bf16[2,4,128,256]{3,2,1,0:T(8,128)(2,1)} collective-permute-done((bf16[2,4,128,256]{3,2,1,0:T(8,128)(2,1)}, bf16[2,4,128,256]{3,2,1,0:T(8,128)(2,1)}, u32[]{:S(2)}, u32[]{:S(2)}) %collective-permute-start.9) | collective-permute-done | bytes 524320 | tf_op jit(solution)/shard_map/ppermute | solution.py:40
  296.2 15.3 %attention.7 = (bf16[512,256]{1,0:T(8,128)(2,1)}, bf16[512,256]{1,0:T(8,128)(2,1)}, bf16[2,4,128,256]{3,2,1,0:T(8,128)(2,1)}, bf16[2,4,128,256]{3,2,1,0:T(8,128)...) custom-call(s32[4,8]{1,0:T(4,128)} %multiply_add_fusion.slot_ref, ...), custom_call_target="tpu_custom_call" | custom-call | flops 3221225472 | bytes 8388608 | tf_op jit(solution)/shard_map/attention/pallas_call | solution.py:200
  326.3 22.8 %collective-permute-done.56.refs_7_ = bf16[2,4,128,256]{3,2,1,0:T(8,128)(2,1)} collective-permute-done((bf16[2,4,128,256]{3,2,1,0:T(8,128)(2,1)}, bf16[2,4,128,256]{3,2,1,0:T(8,128)(2,1)}, u32[]{:S(2)}, u32[]{:S(2)}) %collective-permute-start.56) | collective-permute-done | bytes 524320 | tf_op jit(solution)/shard_map/ppermute | solution.py:40
  349.2 15.2 %attention.6 = (bf16[512,256]{1,0:T(8,128)(2,1)}, bf16[512,256]{1,0:T(8,128)(2,1)}, bf16[2,4,128,256]{3,2,1,0:T(8,128)(2,1)}, bf16[2,4,128,256]{3,2,1,0:T(8,128)...) custom-call(s32[4,8]{1,0:T(4,128)} %get-tuple-element.180.slot_ref, ...), custom_call_target="tpu_custom_call" | custom-call | flops 3221225472 | bytes 8388608 | tf_op jit(solution)/shard_map/attention/pallas_call | solution.py:200
  379.5 11.7 %collective-permute-done.76.refs_7_ = bf16[2,4,128,256]{3,2,1,0:T(8,128)(2,1)} collective-permute-done((bf16[2,4,128,256]{3,2,1,0:T(8,128)(2,1)}, bf16[2,4,128,256]{3,2,1,0:T(8,128)(2,1)}, u32[]{:S(2)}, u32[]{:S(2)}) %collective-permute-start.76) | collective-permute-done | bytes 524320 | tf_op jit(solution)/shard_map/ppermute | solution.py:40
  394.0 15.2 %attention.4 = (bf16[512,256]{1,0:T(8,128)(2,1)}, bf16[512,256]{1,0:T(8,128)(2,1)}, bf16[2,4,128,256]{3,2,1,0:T(8,128)(2,1)}, bf16[2,4,128,256]{3,2,1,0:T(8,128)...) custom-call(s32[4,8]{1,0:T(4,128)} %get-tuple-element.180.slot_ref, ...), custom_call_target="tpu_custom_call" | custom-call | flops 3221225472 | bytes 8388608 | tf_op jit(solution)/shard_map/attention/pallas_call | solution.py:200
  411.1 8.7 %collective-permute-done.62.refs_3_ = bf16[2,4,128,256]{3,2,1,0:T(8,128)(2,1)} collective-permute-done((bf16[2,4,128,256]{3,2,1,0:T(8,128)(2,1)}, bf16[2,4,128,256]{3,2,1,0:T(8,128)(2,1)}, u32[]{:S(2)}, u32[]{:S(2)}) %collective-permute-start.62) | collective-permute-done | bytes 524320 | tf_op jit(solution)/shard_map/ppermute | solution.py:40
  427.5 13.9 %collective-permute-done.66.refs_7_ = bf16[2,4,128,256]{3,2,1,0:T(8,128)(2,1)} collective-permute-done((bf16[2,4,128,256]{3,2,1,0:T(8,128)(2,1)}, bf16[2,4,128,256]{3,2,1,0:T(8,128)(2,1)}, u32[]{:S(2)}, u32[]{:S(2)}) %collective-permute-start.66) | collective-permute-done | bytes 524320 | tf_op jit(solution)/shard_map/ppermute | solution.py:40
  449.2 25.8 %collective-permute-start.57 = (bf16[2,4,128,256]{3,2,1,0:T(8,128)(2,1)}, bf16[2,4,128,256]{3,2,1,0:T(8,128)(2,1)S(1)}, u32[]{:S(2)}, u32[]{:S(2)}) collective-permute-start(bf16[2,4,128,256]{3,2,1,0:T(8,128)(2,1)} %get-tuple-element.153), channel_id=1, source_target_pairs={{0,6},{1,7},{2,0},{3,1},{4,2},{5,3},{6,4},{7,5},{8,14},{9,15},{10,... | collective-permute-start | bytes 1572872 | tf_op jit(solution)/shard_map/ppermute | solution.py:40
  504.6 11.2 %collective-permute-start.68 = (bf16[2,4,128,256]{3,2,1,0:T(8,128)(2,1)}, bf16[2,4,128,256]{3,2,1,0:T(8,128)(2,1)S(1)}, u32[]{:S(2)}, u32[]{:S(2)}) collective-permute-start(bf16[2,4,128,256]{3,2,1,0:T(8,128)(2,1)} %get-tuple-element.166), channel_id=1, source_target_pairs={{0,16},{1,17},{2,18},{3,19},{4,20},{5,21},{6,22},{7,23},{8,24},{9,... | collective-permute-start | bytes 1572872 | tf_op jit(solution)/shard_map/ppermute | solution.py:40
  531.6 8.6 %collective-permute-done.69 = bf16[2,4,128,256]{3,2,1,0:T(8,128)(2,1)S(1)} collective-permute-done((bf16[2,4,128,256]{3,2,1,0:T(8,128)(2,1)}, bf16[2,4,128,256]{3,2,1,0:T(8,128)(2,1)S(1)}, u32[]{:S(2)}, u32[]{:S(2)}) %collective-permute-start.69) | collective-permute-done | bytes 524320 | tf_op jit(solution)/shard_map/ppermute | solution.py:40
  550.6 11.6 %collective-permute-done.49 = bf16[2,4,128,256]{3,2,1,0:T(8,128)(2,1)S(1)} collective-permute-done((bf16[2,4,128,256]{3,2,1,0:T(8,128)(2,1)S(1)}, bf16[2,4,128,256]{3,2,1,0:T(8,128)(2,1)S(1)}, u32[]{:S(2)}, u32[]{:S(2)}) %collective-permute-start.49) | collective-permute-done | bytes 524320 | tf_op jit(solution)/shard_map/ppermute | solution.py:40
  (254 shorter events, 223.6 us)
Async XLA Ops:
  28.7 471.6 %reduce-scatter.7.cloned.1.call-start = ((), (), s32[]{:S(2)}) async-start(), calls=%async_computation.6 | async-start | bytes 589824 | tf_op jit(solution)/shard_map/reduce_scatter | solution.py:289
  35.4 42.3 %collective-permute-start.32 = (bf16[2,4,128,256]{3,2,1,0:T(8,128)(2,1)}, bf16[2,4,128,256]{3,2,1,0:T(8,128)(2,1)}, u32[]{:S(2)}, u32[]{:S(2)}) collective-permute-start(bf16[2,4,128,256]{3,2,1,0:T(8,128)(2,1)} %get-tuple-element.184.refs_0_), channel_id=1, source_target_pairs={{0,6},{1,7},{2,0},{3,1},{4,2},{5,3},{6,4},{7,5},{8,14},{9,15},{10,... | collective-permute-start | bytes 1572872 | tf_op jit(solution)/shard_map/ppermute | solution.py:40
  35.4 50.3 %collective-permute-start.31 = (bf16[2,4,128,256]{3,2,1,0:T(8,128)(2,1)}, bf16[2,4,128,256]{3,2,1,0:T(8,128)(2,1)}, u32[]{:S(2)}, u32[]{:S(2)}) collective-permute-start(bf16[2,4,128,256]{3,2,1,0:T(8,128)(2,1)} %get-tuple-element.184.refs_0_), channel_id=1, source_target_pairs={{0,4},{1,5},{2,6},{3,7},{4,0},{5,1},{6,2},{7,3},{8,12},{9,13},{10,... | collective-permute-start | bytes 1572872 | tf_op jit(solution)/shard_map/ppermute | solution.py:40
  40.3 46.7 %collective-permute-start.30 = (bf16[2,4,128,256]{3,2,1,0:T(8,128)(2,1)}, bf16[2,4,128,256]{3,2,1,0:T(8,128)(2,1)}, u32[]{:S(2)}, u32[]{:S(2)}) collective-permute-start(bf16[2,4,128,256]{3,2,1,0:T(8,128)(2,1)} %get-tuple-element.184.refs_0_), channel_id=1, source_target_pairs={{0,2},{1,3},{2,4},{3,5},{4,6},{5,7},{6,0},{7,1},{8,10},{9,11},{10,... | collective-permute-start | bytes 1572872 | tf_op jit(solution)/shard_map/ppermute | solution.py:40
  43.6 43.4 %collective-permute-start.22 = (bf16[2,4,128,256]{3,2,1,0:T(8,128)(2,1)S(1)}, bf16[2,4,128,256]{3,2,1,0:T(8,128)(2,1)}, u32[]{:S(2)}, u32[]{:S(2)}) collective-permute-start(bf16[2,4,128,256]{3,2,1,0:T(8,128)(2,1)S(1)} %get-tuple-element.185.refs_0_), channel_id=1, source_target_pairs={{0,24},{1,25},{2,26},{3,27},{4,28},{5,29},{6,30},{7,31},{8,0},{9,1... | collective-permute-start | bytes 1572872 | tf_op jit(solution)/shard_map/ppermute | solution.py:40
  99.9 45.7 %collective-permute-start.17 = (bf16[2,4,128,256]{3,2,1,0:T(8,128)(2,1)}, bf16[2,4,128,256]{3,2,1,0:T(8,128)(2,1)S(1)}, u32[]{:S(2)}, u32[]{:S(2)}) collective-permute-start(bf16[2,4,128,256]{3,2,1,0:T(8,128)(2,1)} %get-tuple-element.106), channel_id=1, source_target_pairs={{0,17},{1,16},{2,19},{3,18},{4,21},{5,20},{6,23},{7,22},{8,25},{9,... | collective-permute-start | bytes 1572872 | tf_op jit(solution)/shard_map/ppermute | solution.py:40
  101.6 44.0 %collective-permute-start.18 = (bf16[2,4,128,256]{3,2,1,0:T(8,128)(2,1)}, bf16[2,4,128,256]{3,2,1,0:T(8,128)(2,1)S(1)}, u32[]{:S(2)}, u32[]{:S(2)}) collective-permute-start(bf16[2,4,128,256]{3,2,1,0:T(8,128)(2,1)} %get-tuple-element.107), channel_id=1, source_target_pairs={{0,24},{1,25},{2,26},{3,27},{4,28},{5,29},{6,30},{7,31},{8,0},{9,1... | collective-permute-start | bytes 1572872 | tf_op jit(solution)/shard_map/ppermute | solution.py:40
  197.2 45.8 %collective-permute-start.27 = (bf16[2,4,128,256]{3,2,1,0:T(8,128)(2,1)}, bf16[2,4,128,256]{3,2,1,0:T(8,128)(2,1)}, u32[]{:S(2)}, u32[]{:S(2)}) collective-permute-start(bf16[2,4,128,256]{3,2,1,0:T(8,128)(2,1)} %get-tuple-element.115), channel_id=1, source_target_pairs={{0,5},{1,4},{2,7},{3,6},{4,1},{5,0},{6,3},{7,2},{8,13},{9,12},{10,... | collective-permute-start | bytes 1572872 | tf_op jit(solution)/shard_map/ppermute | solution.py:40
  199.5 43.6 %collective-permute-start.28 = (bf16[2,4,128,256]{3,2,1,0:T(8,128)(2,1)}, bf16[2,4,128,256]{3,2,1,0:T(8,128)(2,1)}, u32[]{:S(2)}, u32[]{:S(2)}) collective-permute-start(bf16[2,4,128,256]{3,2,1,0:T(8,128)(2,1)} %get-tuple-element.116), channel_id=1, source_target_pairs={{0,6},{1,7},{2,0},{3,1},{4,2},{5,3},{6,4},{7,5},{8,14},{9,15},{10,... | collective-permute-start | bytes 1572872 | tf_op jit(solution)/shard_map/ppermute | solution.py:40
  202.8 44.8 %collective-permute-start.29 = (bf16[2,4,128,256]{3,2,1,0:T(8,128)(2,1)}, bf16[2,4,128,256]{3,2,1,0:T(8,128)(2,1)}, u32[]{:S(2)}, u32[]{:S(2)}) collective-permute-start(bf16[2,4,128,256]{3,2,1,0:T(8,128)(2,1)} %get-tuple-element.117), channel_id=1, source_target_pairs={{0,7},{1,6},{2,1},{3,0},{4,3},{5,2},{6,5},{7,4},{8,15},{9,14},{10,... | collective-permute-start | bytes 1572872 | tf_op jit(solution)/shard_map/ppermute | solution.py:40
  249.8 45.9 %collective-permute-start.9 = (bf16[2,4,128,256]{3,2,1,0:T(8,128)(2,1)}, bf16[2,4,128,256]{3,2,1,0:T(8,128)(2,1)}, u32[]{:S(2)}, u32[]{:S(2)}) collective-permute-start(bf16[2,4,128,256]{3,2,1,0:T(8,128)(2,1)} %get-tuple-element.99), channel_id=1, source_target_pairs={{0,7},{1,6},{2,1},{3,0},{4,3},{5,2},{6,5},{7,4},{8,15},{9,14},{10,... | collective-permute-start | bytes 1572872 | tf_op jit(solution)/shard_map/ppermute | solution.py:40
  253.7 246.7 %reduce-scatter.11.cloned.1.call-start = ((), (), s32[]{:S(2)}) async-start(), calls=%async_computation.8 | async-start | bytes 589824 | tf_op jit(solution)/shard_map/reduce_scatter | solution.py:289
  258.7 52.8 %collective-permute-start.50 = (bf16[2,4,128,256]{3,2,1,0:T(8,128)(2,1)}, bf16[2,4,128,256]{3,2,1,0:T(8,128)(2,1)}, u32[]{:S(2)}, u32[]{:S(2)}) collective-permute-start(bf16[2,4,128,256]{3,2,1,0:T(8,128)(2,1)} %get-tuple-element.145), channel_id=1, source_target_pairs={{0,1},{1,0},{2,3},{3,2},{4,5},{5,4},{6,7},{7,6},{8,9},{9,8},{10,11... | collective-permute-start | bytes 1572872 | tf_op jit(solution)/shard_map/ppermute | solution.py:40
  316.8 183.6 %reduce-scatter.9.cloned.1.call-start = ((), (), s32[]{:S(2)}) async-start(), calls=%async_computation.7 | async-start | bytes 589824 | tf_op jit(solution)/shard_map/reduce_scatter | solution.py:289
  316.8 47.6 %collective-permute-start.70 = (bf16[2,4,128,256]{3,2,1,0:T(8,128)(2,1)}, bf16[2,4,128,256]{3,2,1,0:T(8,128)(2,1)}, u32[]{:S(2)}, u32[]{:S(2)}) collective-permute-start(bf16[2,4,128,256]{3,2,1,0:T(8,128)(2,1)} %get-tuple-element.169), channel_id=1, source_target_pairs={{0,1},{1,0},{2,3},{3,2},{4,5},{5,4},{6,7},{7,6},{8,9},{9,8},{10,11... | collective-permute-start | bytes 1572872 | tf_op jit(solution)/shard_map/ppermute | solution.py:40
  316.9 48.0 %collective-permute-start.71 = (bf16[2,4,128,256]{3,2,1,0:T(8,128)(2,1)}, bf16[2,4,128,256]{3,2,1,0:T(8,128)(2,1)}, u32[]{:S(2)}, u32[]{:S(2)}) collective-permute-start(bf16[2,4,128,256]{3,2,1,0:T(8,128)(2,1)} %get-tuple-element.170), channel_id=1, source_target_pairs={{0,24},{1,25},{2,26},{3,27},{4,28},{5,29},{6,30},{7,31},{8,0},{9,1... | collective-permute-start | bytes 1572872 | tf_op jit(solution)/shard_map/ppermute | solution.py:40
  318.0 49.7 %collective-permute-start.72 = (bf16[2,4,128,256]{3,2,1,0:T(8,128)(2,1)}, bf16[2,4,128,256]{3,2,1,0:T(8,128)(2,1)}, u32[]{:S(2)}, u32[]{:S(2)}) collective-permute-start(bf16[2,4,128,256]{3,2,1,0:T(8,128)(2,1)} %get-tuple-element.171), channel_id=1, source_target_pairs={{0,25},{1,24},{2,27},{3,26},{4,29},{5,28},{6,31},{7,30},{8,1},{9,0... | collective-permute-start | bytes 1572872 | tf_op jit(solution)/shard_map/ppermute | solution.py:40
  325.5 44.5 %collective-permute-start.73 = (bf16[2,4,128,256]{3,2,1,0:T(8,128)(2,1)}, bf16[2,4,128,256]{3,2,1,0:T(8,128)(2,1)}, u32[]{:S(2)}, u32[]{:S(2)}) collective-permute-start(bf16[2,4,128,256]{3,2,1,0:T(8,128)(2,1)} %get-tuple-element.172), channel_id=1, source_target_pairs={{0,16},{1,17},{2,18},{3,19},{4,20},{5,21},{6,22},{7,23},{8,24},{9,... | collective-permute-start | bytes 1572872 | tf_op jit(solution)/shard_map/ppermute | solution.py:40
  369.9 130.4 %reduce-scatter.5.cloned.1.call-start = ((), (), s32[]{:S(2)}) async-start(), calls=%async_computation.5 | async-start | bytes 589824 | tf_op jit(solution)/shard_map/reduce_scatter | solution.py:289
  373.4 46.4 %collective-permute-start.62 = (bf16[2,4,128,256]{3,2,1,0:T(8,128)(2,1)}, bf16[2,4,128,256]{3,2,1,0:T(8,128)(2,1)}, u32[]{:S(2)}, u32[]{:S(2)}) collective-permute-start(bf16[2,4,128,256]{3,2,1,0:T(8,128)(2,1)} %get-tuple-element.159), channel_id=1, source_target_pairs={{0,7},{1,6},{2,1},{3,0},{4,3},{5,2},{6,5},{7,4},{8,15},{9,14},{10,... | collective-permute-start | bytes 1572872 | tf_op jit(solution)/shard_map/ppermute | solution.py:40
  378.0 43.8 %collective-permute-start.63 = (bf16[2,4,128,256]{3,2,1,0:T(8,128)(2,1)}, bf16[2,4,128,256]{3,2,1,0:T(8,128)(2,1)}, u32[]{:S(2)}, u32[]{:S(2)}) collective-permute-start(bf16[2,4,128,256]{3,2,1,0:T(8,128)(2,1)} %get-tuple-element.160), channel_id=1, source_target_pairs={{0,4},{1,5},{2,6},{3,7},{4,0},{5,1},{6,2},{7,3},{8,12},{9,13},{10,... | collective-permute-start | bytes 1572872 | tf_op jit(solution)/shard_map/ppermute | solution.py:40
  425.0 50.1 %collective-permute-start.43 = (bf16[2,4,128,256]{3,2,1,0:T(8,128)(2,1)}, bf16[2,4,128,256]{3,2,1,0:T(8,128)(2,1)}, u32[]{:S(2)}, u32[]{:S(2)}) collective-permute-start(bf16[2,4,128,256]{3,2,1,0:T(8,128)(2,1)} %get-tuple-element.136), channel_id=1, source_target_pairs={{0,4},{1,5},{2,6},{3,7},{4,0},{5,1},{6,2},{7,3},{8,12},{9,13},{10,... | collective-permute-start | bytes 1572872 | tf_op jit(solution)/shard_map/ppermute | solution.py:40
  441.4 51.0 %collective-permute-start.46 = (bf16[2,4,128,256]{3,2,1,0:T(8,128)(2,1)}, bf16[2,4,128,256]{3,2,1,0:T(8,128)(2,1)}, u32[]{:S(2)}, u32[]{:S(2)}) collective-permute-start(bf16[2,4,128,256]{3,2,1,0:T(8,128)(2,1)} %get-tuple-element.139), channel_id=1, source_target_pairs={{0,3},{1,2},{2,5},{3,4},{4,7},{5,6},{6,1},{7,0},{8,11},{9,10},{10,... | collective-permute-start | bytes 1572872 | tf_op jit(solution)/shard_map/ppermute | solution.py:40
  449.2 49.6 %collective-permute-start.57 = (bf16[2,4,128,256]{3,2,1,0:T(8,128)(2,1)}, bf16[2,4,128,256]{3,2,1,0:T(8,128)(2,1)S(1)}, u32[]{:S(2)}, u32[]{:S(2)}) collective-permute-start(bf16[2,4,128,256]{3,2,1,0:T(8,128)(2,1)} %get-tuple-element.153), channel_id=1, source_target_pairs={{0,6},{1,7},{2,0},{3,1},{4,2},{5,3},{6,4},{7,5},{8,14},{9,15},{10,... | collective-permute-start | bytes 1572872 | tf_op jit(solution)/shard_map/ppermute | solution.py:40
  (88 other events, 2585.8 us)
Sparse Core Ops, SparseCore 0:
  253.8 41.0 reduce-scatter.6
  316.9 29.1 reduce-scatter.10
  370.1 52.3 reduce-scatter.8
  427.6 51.8 reduce-scatter.4

commit v3 on v2

--- a/solution.py
+++ b/solution.py
@@ -21,7 +21,6 @@
 LOCAL = 4
 DESTS = 8
 masked_score = -1e30
-ROWS = [[y * NZ * NCORE + i for i in range(NZ * NCORE)] for y in range(NY)]
 
 
 def shift(dy, dz, dc):
@@ -280,19 +279,16 @@
             return move(x, 0, step, core) if along_y else move(x, step, 0, core)
 
         mine = own_tiles[..., chunk * COLS : (chunk + 1) * COLS]
+        if chunk == 2:
+            mine, told = lax.optimization_barrier((mine, told))
         held = [near_move(mine, k) for k in range(4)]
         packed = pack(jnp.maximum(asked[kind], 0), held)
         tiles = [far_move(packed[d], d, 1) for d in range(DESTS)]
         out, d_query, grads = attention(chunk, slots[kind], tile_count, queries, d_attended, tiles)
-        product = dot(out, out_grad, 0, 0).astype(jnp.bfloat16)
         partials.append(
-            lax.psum_scatter(
-                product,
-                "seq",
-                scatter_dimension=0,
-                axis_index_groups=ROWS,
-                tiled=True,
-            )
+            dot(out, out_grad, 0, 0)
+            .astype(jnp.bfloat16)
+            .reshape(NZ, NCORE, COLS // DESTS, D)
         )
         attended.append(out)
         d_queries.append(d_query)
@@ -304,8 +300,16 @@
     attended = jnp.concatenate(attended, axis=1)
     joined = jnp.dot(attended, out_weight, preferred_element_type=jnp.float32).astype(jnp.bfloat16)
     partials = jnp.stack(partials)
+    across = []
+    for d in range(DESTS):
+        to_z, to_core = (z + d // NCORE) % NZ, c ^ (d % NCORE)
+        piece = lax.dynamic_slice(
+            partials, (0, to_z, to_core, 0, 0), (NY, 1, 1) + partials.shape[3:]
+        ).reshape((NY,) + partials.shape[3:])
+        across.append(move(piece, 0, d // NCORE, d % NCORE))
+    row = sum(part.astype(jnp.float32) for part in across).astype(jnp.bfloat16)
     arrived = [
-        move(lax.dynamic_index_in_dim(partials, (y - k) % NY, 0, keepdims=False), -k, 0, 0)
+        move(lax.dynamic_index_in_dim(row, (y - k) % NY, 0, keepdims=False), -k, 0, 0)
         for k in range(NY)
     ]
     d_out_weight = sum(part.astype(jnp.float32) for part in arrived)

time: 581 us -> 636 us (1.095)
  the two profiles are of different devices: /device:TPU:1 before, /device:TPU:0 now
where the time goes in v3:
time: 636 us; the launch traced here: 627 us
  waiting for transfers between devices  342 us (54%)
  starting transfers between devices  152 us (24%)
  Pallas kernels  98 us (15%)
  other arithmetic  14.8 us (2%)
  matrix products  9.22 us (1%)
  local copies, waits for them, and re-layouts  9.21 us (1%)
    ppermute x90, waiting for transfers between devices, move(): return lax.ppermute(x, 'seq', shift(dy, dz, dc))  326 us
    ppermute x90, starting transfers between devices, move(): return lax.ppermute(x, 'seq', shift(dy, dz, dc))  145 us
    pallas_call x4, Pallas kernels, attention(): pl.pallas_call(functools.partial(attention_kernel, blocks), grid_spec=plt...  61.6 us
    pallas_call x4, Pallas kernels, merge(): pl.pallas_call(merge_kernel, grid_spec=pltpu.PrefetchScalarGridSpec(num_s...  18.3 us
    pallas_call x4, Pallas kernels, pack(): pl.pallas_call(pack_kernel, grid_spec=pltpu.PrefetchScalarGridSpec(num_sc...  18.1 us
    all_to_all x1, waiting for transfers between devices, local(): lax.all_to_all(along.reshape(devices, NY + NZ), 'seq', 0, 0, tiled=True)  15.3 us
  transfers between devices with their start and end apart: 91, of which 36 were waited for; matrix products, arithmetic and copies ran while one was open for 4% of the time, Pallas kernels for 13%

profile of v3, /device:TPU:0, one launch (start us, length us, event | category | flops | bytes accessed | tf_op | source)
XLA Modules:
  0.0 626.5 jit_solution(5088037641230153550)
XLA Ops:
  21.1 15.3 %all-to-all-done = s32[32,1,8]{2,1,0:T(1,128)S(1)} async-done(((s32[32,1,8]{2,1,0:T(1,128)}), s32[32,1,8]{2,1,0:T(1,128)S(1)}, u32[]{:S(2)}, u32[]{:S(2)}) %all-to-all-start) | async-done | bytes 1056 | tf_op jit(solution)/shard_map/all_to_all | solution.py:248
  45.5 30.5 %collective-permute-done.10.refs_1_ = bf16[2,4,128,256]{3,2,1,0:T(8,128)(2,1)} collective-permute-done((bf16[2,4,128,256]{3,2,1,0:T(8,128)(2,1)}, bf16[2,4,128,256]{3,2,1,0:T(8,128)(2,1)}, u32[]{:S(2)}, u32[]{:S(2)}) %collective-permute-start.10) | collective-permute-done | bytes 524320 | tf_op jit(solution)/shard_map/ppermute | solution.py:39
  94.7 8.3 %collective-permute-done.20.refs_1_ = bf16[2,4,128,256]{3,2,1,0:T(8,128)(2,1)} collective-permute-done((bf16[2,4,128,256]{3,2,1,0:T(8,128)(2,1)}, bf16[2,4,128,256]{3,2,1,0:T(8,128)(2,1)}, u32[]{:S(2)}, u32[]{:S(2)}) %collective-permute-start.20) | collective-permute-done | bytes 524320 | tf_op jit(solution)/shard_map/ppermute | solution.py:39
  104.5 9.8 %collective-permute-done.14.refs_2_ = bf16[2,4,128,256]{3,2,1,0:T(8,128)(2,1)} collective-permute-done((bf16[2,4,128,256]{3,2,1,0:T(8,128)(2,1)}, bf16[2,4,128,256]{3,2,1,0:T(8,128)(2,1)}, u32[]{:S(2)}, u32[]{:S(2)}) %collective-permute-start.14) | collective-permute-done | bytes 524320 | tf_op jit(solution)/shard_map/ppermute | solution.py:39
  114.2 11.8 %collective-permute-done.15.refs_3_ = bf16[2,4,128,256]{3,2,1,0:T(8,128)(2,1)} collective-permute-done((bf16[2,4,128,256]{3,2,1,0:T(8,128)(2,1)}, bf16[2,4,128,256]{3,2,1,0:T(8,128)(2,1)}, u32[]{:S(2)}, u32[]{:S(2)}) %collective-permute-start.15) | collective-permute-done | bytes 524320 | tf_op jit(solution)/shard_map/ppermute | solution.py:39
  126.2 11.4 %collective-permute-done.16.refs_4_ = bf16[2,4,128,256]{3,2,1,0:T(8,128)(2,1)} collective-permute-done((bf16[2,4,128,256]{3,2,1,0:T(8,128)(2,1)}, bf16[2,4,128,256]{3,2,1,0:T(8,128)(2,1)}, u32[]{:S(2)}, u32[]{:S(2)}) %collective-permute-start.16) | collective-permute-done | bytes 524320 | tf_op jit(solution)/shard_map/ppermute | solution.py:39
  137.6 9.4 %collective-permute-done.17.refs_5_ = bf16[2,4,128,256]{3,2,1,0:T(8,128)(2,1)} collective-permute-done((bf16[2,4,128,256]{3,2,1,0:T(8,128)(2,1)}, bf16[2,4,128,256]{3,2,1,0:T(8,128)(2,1)}, u32[]{:S(2)}, u32[]{:S(2)}) %collective-permute-start.17) | collective-permute-done | bytes 524320 | tf_op jit(solution)/shard_map/ppermute | solution.py:39
  171.2 11.4 %collective-permute-done.36.refs_4_ = bf16[2,4,128,256]{3,2,1,0:T(8,128)(2,1)} collective-permute-done((bf16[2,4,128,256]{3,2,1,0:T(8,128)(2,1)}, bf16[2,4,128,256]{3,2,1,0:T(8,128)(2,1)}, u32[]{:S(2)}, u32[]{:S(2)}) %collective-permute-start.36) | collective-permute-done | bytes 524320 | tf_op jit(solution)/shard_map/ppermute | solution.py:39
  193.3 15.4 %attention.5 = (bf16[512,256]{1,0:T(8,128)(2,1)}, bf16[512,256]{1,0:T(8,128)(2,1)}, bf16[2,4,128,256]{3,2,1,0:T(8,128)(2,1)}, bf16[2,4,128,256]{3,2,1,0:T(8,128)...) custom-call(s32[4,8]{1,0:T(4,128)} %multiply_add_fusion.slot_ref, ...), custom_call_target="tpu_custom_call" | custom-call | flops 3221225472 | bytes 8388608 | tf_op jit(solution)/shard_map/attention/pallas_call | solution.py:199
  214.5 15.4 %attention.7 = (bf16[512,256]{1,0:T(8,128)(2,1)}, bf16[512,256]{1,0:T(8,128)(2,1)}, bf16[2,4,128,256]{3,2,1,0:T(8,128)(2,1)}, bf16[2,4,128,256]{3,2,1,0:T(8,128)...) custom-call(s32[4,8]{1,0:T(4,128)} %multiply_add_fusion.slot_ref, ...), custom_call_target="tpu_custom_call" | custom-call | flops 3221225472 | bytes 8388608 | tf_op jit(solution)/shard_map/attention/pallas_call | solution.py:199
  238.9 8.1 %collective-permute-done.9.refs_7_ = bf16[2,4,128,256]{3,2,1,0:T(8,128)(2,1)} collective-permute-done((bf16[2,4,128,256]{3,2,1,0:T(8,128)(2,1)S(1)}, bf16[2,4,128,256]{3,2,1,0:T(8,128)(2,1)}, u32[]{:S(2)}, u32[]{:S(2)}) %collective-permute-start.9) | collective-permute-done | bytes 524320 | tf_op jit(solution)/shard_map/ppermute | solution.py:39
  250.1 15.5 %attention.4 = (bf16[512,256]{1,0:T(8,128)(2,1)}, bf16[512,256]{1,0:T(8,128)(2,1)}, bf16[2,4,128,256]{3,2,1,0:T(8,128)(2,1)}, bf16[2,4,128,256]{3,2,1,0:T(8,128)...) custom-call(s32[4,8]{1,0:T(4,128)} %get-tuple-element.182.slot_ref, ...), custom_call_target="tpu_custom_call" | custom-call | flops 3221225472 | bytes 8388608 | tf_op jit(solution)/shard_map/attention/pallas_call | solution.py:199
  268.9 9.9 %collective-permute-done.25.refs_3_ = bf16[2,4,128,256]{3,2,1,0:T(8,128)(2,1)} collective-permute-done((bf16[2,4,128,256]{3,2,1,0:T(8,128)(2,1)S(1)}, bf16[2,4,128,256]{3,2,1,0:T(8,128)(2,1)}, u32[]{:S(2)}, u32[]{:S(2)}) %collective-permute-start.25) | collective-permute-done | bytes 524320 | tf_op jit(solution)/shard_map/ppermute | solution.py:39
  280.9 10.9 %collective-permute-done.29.refs_7_ = bf16[2,4,128,256]{3,2,1,0:T(8,128)(2,1)S(1)} collective-permute-done((bf16[2,4,128,256]{3,2,1,0:T(8,128)(2,1)S(1)}, bf16[2,4,128,256]{3,2,1,0:T(8,128)(2,1)S(1)}, u32[]{:S(2)}, u32[]{:S(2)}) %collective-permute-start.29) | collective-permute-done | bytes 524320 | tf_op jit(solution)/shard_map/ppermute | solution.py:39
  292.7 15.3 %attention.6 = (bf16[512,256]{1,0:T(8,128)(2,1)}, bf16[512,256]{1,0:T(8,128)(2,1)}, bf16[2,4,128,256]{3,2,1,0:T(8,128)(2,1)}, bf16[2,4,128,256]{3,2,1,0:T(8,128)...) custom-call(s32[4,8]{1,0:T(4,128)} %get-tuple-element.182.slot_ref, ...), custom_call_target="tpu_custom_call" | custom-call | flops 3221225472 | bytes 8388608 | tf_op jit(solution)/shard_map/attention/pallas_call | solution.py:199
  365.9 22.8 %collective-permute-start.70 = (bf16[2,4,128,256]{3,2,1,0:T(8,128)(2,1)}, bf16[2,4,128,256]{3,2,1,0:T(8,128)(2,1)}, u32[]{:S(2)}, u32[]{:S(2)}) collective-permute-start(bf16[2,4,128,256]{3,2,1,0:T(8,128)(2,1)} %get-tuple-element.171), channel_id=1, source_target_pairs={{0,1},{1,0},{2,3},{3,2},{4,5},{5,4},{6,7},{7,6},{8,9},{9,8},{10,11... | collective-permute-start | bytes 1572872 | tf_op jit(solution)/shard_map/ppermute | solution.py:39
  394.7 9.3 %collective-permute-done.56.refs_7_ = bf16[2,4,128,256]{3,2,1,0:T(8,128)(2,1)} collective-permute-done((bf16[2,4,128,256]{3,2,1,0:T(8,128)(2,1)S(1)}, bf16[2,4,128,256]{3,2,1,0:T(8,128)(2,1)}, u32[]{:S(2)}, u32[]{:S(2)}) %collective-permute-start.56) | collective-permute-done | bytes 524320 | tf_op jit(solution)/shard_map/ppermute | solution.py:39
  406.9 31.2 %collective-permute-done.72.refs_3_ = bf16[2,4,128,256]{3,2,1,0:T(8,128)(2,1)} collective-permute-done((bf16[2,4,128,256]{3,2,1,0:T(8,128)(2,1)}, bf16[2,4,128,256]{3,2,1,0:T(8,128)(2,1)}, u32[]{:S(2)}, u32[]{:S(2)}) %collective-permute-start.72) | collective-permute-done | bytes 524320 | tf_op jit(solution)/shard_map/ppermute | solution.py:39
  455.7 33.2 %collective-permute-done.42.refs_3_ = bf16[2,4,128,256]{3,2,1,0:T(8,128)(2,1)} collective-permute-done((bf16[2,4,128,256]{3,2,1,0:T(8,128)(2,1)}, bf16[2,4,128,256]{3,2,1,0:T(8,128)(2,1)}, u32[]{:S(2)}, u32[]{:S(2)}) %collective-permute-start.42) | collective-permute-done | bytes 524320 | tf_op jit(solution)/shard_map/ppermute | solution.py:39
  505.1 33.0 %collective-permute-done.62.refs_3_ = bf16[2,4,128,256]{3,2,1,0:T(8,128)(2,1)} collective-permute-done((bf16[2,4,128,256]{3,2,1,0:T(8,128)(2,1)}, bf16[2,4,128,256]{3,2,1,0:T(8,128)(2,1)}, u32[]{:S(2)}, u32[]{:S(2)}) %collective-permute-start.62) | collective-permute-done | bytes 524320 | tf_op jit(solution)/shard_map/ppermute | solution.py:39
  575.0 12.0 %collective-permute-done.77 = bf16[2,4,128,256]{3,2,1,0:T(8,128)(2,1)} collective-permute-done((bf16[2,4,128,256]{3,2,1,0:T(8,128)(2,1)}, bf16[2,4,128,256]{3,2,1,0:T(8,128)(2,1)}, u32[]{:S(2)}, u32[]{:S(2)}) %collective-permute-start.77) | collective-permute-done | bytes 524320 | tf_op jit(solution)/shard_map/ppermute | solution.py:39
  596.1 8.1 %collective-permute-done.49 = bf16[2,4,128,256]{3,2,1,0:T(8,128)(2,1)S(1)} collective-permute-done((bf16[2,4,128,256]{3,2,1,0:T(8,128)(2,1)}, bf16[2,4,128,256]{3,2,1,0:T(8,128)(2,1)S(1)}, u32[]{:S(2)}, u32[]{:S(2)}) %collective-permute-start.49) | collective-permute-done | bytes 524320 | tf_op jit(solution)/shard_map/ppermute | solution.py:39
  605.5 8.4 %collective-permute-done.67 = bf16[2,4,128,256]{3,2,1,0:T(8,128)(2,1)S(1)} collective-permute-done((bf16[2,4,128,256]{3,2,1,0:T(8,128)(2,1)S(1)}, bf16[2,4,128,256]{3,2,1,0:T(8,128)(2,1)S(1)}, u32[]{:S(2)}, u32[]{:S(2)}) %collective-permute-start.67) | collective-permute-done | bytes 524320 | tf_op jit(solution)/shard_map/ppermute | solution.py:39
  615.5 9.0 %collective-permute-done.69 = bf16[2,4,128,256]{3,2,1,0:T(8,128)(2,1)S(1)} collective-permute-done((bf16[2,4,128,256]{3,2,1,0:T(8,128)(2,1)S(1)}, bf16[2,4,128,256]{3,2,1,0:T(8,128)(2,1)S(1)}, u32[]{:S(2)}, u32[]{:S(2)}) %collective-permute-start.69) | collective-permute-done | bytes 524320 | tf_op jit(solution)/shard_map/ppermute | solution.py:39
  (300 shorter events, 259.5 us)
Async XLA Ops:
  36.4 46.2 %collective-permute-start.32 = (bf16[2,4,128,256]{3,2,1,0:T(8,128)(2,1)}, bf16[2,4,128,256]{3,2,1,0:T(8,128)(2,1)}, u32[]{:S(2)}, u32[]{:S(2)}) collective-permute-start(bf16[2,4,128,256]{3,2,1,0:T(8,128)(2,1)} %get-tuple-element.193.refs_0_), channel_id=1, source_target_pairs={{0,6},{1,7},{2,0},{3,1},{4,2},{5,3},{6,4},{7,5},{8,14},{9,15},{10,... | collective-permute-start | bytes 1572872 | tf_op jit(solution)/shard_map/ppermute | solution.py:39
  38.1 45.6 %collective-permute-start.31 = (bf16[2,4,128,256]{3,2,1,0:T(8,128)(2,1)}, bf16[2,4,128,256]{3,2,1,0:T(8,128)(2,1)}, u32[]{:S(2)}, u32[]{:S(2)}) collective-permute-start(bf16[2,4,128,256]{3,2,1,0:T(8,128)(2,1)} %get-tuple-element.193.refs_0_), channel_id=1, source_target_pairs={{0,4},{1,5},{2,6},{3,7},{4,0},{5,1},{6,2},{7,3},{8,12},{9,13},{10,... | collective-permute-start | bytes 1572872 | tf_op jit(solution)/shard_map/ppermute | solution.py:39
  39.4 44.3 %collective-permute-start.30 = (bf16[2,4,128,256]{3,2,1,0:T(8,128)(2,1)}, bf16[2,4,128,256]{3,2,1,0:T(8,128)(2,1)}, u32[]{:S(2)}, u32[]{:S(2)}) collective-permute-start(bf16[2,4,128,256]{3,2,1,0:T(8,128)(2,1)} %get-tuple-element.193.refs_0_), channel_id=1, source_target_pairs={{0,2},{1,3},{2,4},{3,5},{4,6},{5,7},{6,0},{7,1},{8,10},{9,11},{10,... | collective-permute-start | bytes 1572872 | tf_op jit(solution)/shard_map/ppermute | solution.py:39
  41.6 42.7 %collective-permute-start.22 = (bf16[2,4,128,256]{3,2,1,0:T(8,128)(2,1)}, bf16[2,4,128,256]{3,2,1,0:T(8,128)(2,1)}, u32[]{:S(2)}, u32[]{:S(2)}) collective-permute-start(bf16[2,4,128,256]{3,2,1,0:T(8,128)(2,1)} %get-tuple-element.111.refs_0_), channel_id=1, source_target_pairs={{0,24},{1,25},{2,26},{3,27},{4,28},{5,29},{6,30},{7,31},{8,0},{9,1... | collective-permute-start | bytes 1572872 | tf_op jit(solution)/shard_map/ppermute | solution.py:39
  92.7 44.9 %collective-permute-start.16 = (bf16[2,4,128,256]{3,2,1,0:T(8,128)(2,1)}, bf16[2,4,128,256]{3,2,1,0:T(8,128)(2,1)}, u32[]{:S(2)}, u32[]{:S(2)}) collective-permute-start(bf16[2,4,128,256]{3,2,1,0:T(8,128)(2,1)} %get-tuple-element.106), channel_id=1, source_target_pairs={{0,16},{1,17},{2,18},{3,19},{4,20},{5,21},{6,22},{7,23},{8,24},{9,... | collective-permute-start | bytes 1572872 | tf_op jit(solution)/shard_map/ppermute | solution.py:39
  103.0 44.0 %collective-permute-start.17 = (bf16[2,4,128,256]{3,2,1,0:T(8,128)(2,1)}, bf16[2,4,128,256]{3,2,1,0:T(8,128)(2,1)}, u32[]{:S(2)}, u32[]{:S(2)}) collective-permute-start(bf16[2,4,128,256]{3,2,1,0:T(8,128)(2,1)} %get-tuple-element.107), channel_id=1, source_target_pairs={{0,17},{1,16},{2,19},{3,18},{4,21},{5,20},{6,23},{7,22},{8,25},{9,... | collective-permute-start | bytes 1572872 | tf_op jit(solution)/shard_map/ppermute | solution.py:39
  104.3 42.7 %collective-permute-start.18 = (bf16[2,4,128,256]{3,2,1,0:T(8,128)(2,1)}, bf16[2,4,128,256]{3,2,1,0:T(8,128)(2,1)}, u32[]{:S(2)}, u32[]{:S(2)}) collective-permute-start(bf16[2,4,128,256]{3,2,1,0:T(8,128)(2,1)} %get-tuple-element.108), channel_id=1, source_target_pairs={{0,24},{1,25},{2,26},{3,27},{4,28},{5,29},{6,30},{7,31},{8,0},{9,1... | collective-permute-start | bytes 1572872 | tf_op jit(solution)/shard_map/ppermute | solution.py:39
  148.6 43.3 %collective-permute-start.37 = (bf16[2,4,128,256]{3,2,1,0:T(8,128)(2,1)}, bf16[2,4,128,256]{3,2,1,0:T(8,128)(2,1)}, u32[]{:S(2)}, u32[]{:S(2)}) collective-permute-start(bf16[2,4,128,256]{3,2,1,0:T(8,128)(2,1)} %get-tuple-element.126), channel_id=1, source_target_pairs={{0,17},{1,16},{2,19},{3,18},{4,21},{5,20},{6,23},{7,22},{8,25},{9,... | collective-permute-start | bytes 1572872 | tf_op jit(solution)/shard_map/ppermute | solution.py:39
  161.7 47.1 %collective-permute-start.39 = (bf16[2,4,128,256]{3,2,1,0:T(8,128)(2,1)}, bf16[2,4,128,256]{3,2,1,0:T(8,128)(2,1)}, u32[]{:S(2)}, u32[]{:S(2)}) collective-permute-start(bf16[2,4,128,256]{3,2,1,0:T(8,128)(2,1)} %get-tuple-element.128), channel_id=1, source_target_pairs={{0,25},{1,24},{2,27},{3,26},{4,29},{5,28},{6,31},{7,30},{8,1},{9,0... | collective-permute-start | bytes 1572872 | tf_op jit(solution)/shard_map/ppermute | solution.py:39
  232.2 46.6 %collective-permute-start.25 = (bf16[2,4,128,256]{3,2,1,0:T(8,128)(2,1)S(1)}, bf16[2,4,128,256]{3,2,1,0:T(8,128)(2,1)}, u32[]{:S(2)}, u32[]{:S(2)}) collective-permute-start(bf16[2,4,128,256]{3,2,1,0:T(8,128)(2,1)S(1)} %copy-done.33), channel_id=1, source_target_pairs={{0,3},{1,2},{2,5},{3,4},{4,7},{5,6},{6,1},{7,0},{8,11},{9,10},{10,... | collective-permute-start | bytes 1572872 | tf_op jit(solution)/shard_map/ppermute | solution.py:39
  236.1 42.7 %collective-permute-start.26 = (bf16[2,4,128,256]{3,2,1,0:T(8,128)(2,1)S(1)}, bf16[2,4,128,256]{3,2,1,0:T(8,128)(2,1)}, u32[]{:S(2)}, u32[]{:S(2)}) collective-permute-start(bf16[2,4,128,256]{3,2,1,0:T(8,128)(2,1)S(1)} %copy-done.32), channel_id=1, source_target_pairs={{0,4},{1,5},{2,6},{3,7},{4,0},{5,1},{6,2},{7,3},{8,12},{9,13},{10,... | collective-permute-start | bytes 1572872 | tf_op jit(solution)/shard_map/ppermute | solution.py:39
  358.0 46.0 %collective-permute-start.56 = (bf16[2,4,128,256]{3,2,1,0:T(8,128)(2,1)S(1)}, bf16[2,4,128,256]{3,2,1,0:T(8,128)(2,1)}, u32[]{:S(2)}, u32[]{:S(2)}) collective-permute-start(bf16[2,4,128,256]{3,2,1,0:T(8,128)(2,1)S(1)} %copy-done.27), channel_id=1, source_target_pairs={{0,9},{1,8},{2,11},{3,10},{4,13},{5,12},{6,15},{7,14},{8,17},{9,16... | collective-permute-start | bytes 1572872 | tf_op jit(solution)/shard_map/ppermute | solution.py:39
  392.3 45.9 %collective-permute-start.72 = (bf16[2,4,128,256]{3,2,1,0:T(8,128)(2,1)}, bf16[2,4,128,256]{3,2,1,0:T(8,128)(2,1)}, u32[]{:S(2)}, u32[]{:S(2)}) collective-permute-start(bf16[2,4,128,256]{3,2,1,0:T(8,128)(2,1)} %get-tuple-element.173), channel_id=1, source_target_pairs={{0,25},{1,24},{2,27},{3,26},{4,29},{5,28},{6,31},{7,30},{8,1},{9,0... | collective-permute-start | bytes 1572872 | tf_op jit(solution)/shard_map/ppermute | solution.py:39
  392.7 45.5 %collective-permute-start.73 = (bf16[2,4,128,256]{3,2,1,0:T(8,128)(2,1)}, bf16[2,4,128,256]{3,2,1,0:T(8,128)(2,1)}, u32[]{:S(2)}, u32[]{:S(2)}) collective-permute-start(bf16[2,4,128,256]{3,2,1,0:T(8,128)(2,1)} %get-tuple-element.174), channel_id=1, source_target_pairs={{0,16},{1,17},{2,18},{3,19},{4,20},{5,21},{6,22},{7,23},{8,24},{9,... | collective-permute-start | bytes 1572872 | tf_op jit(solution)/shard_map/ppermute | solution.py:39
  406.7 42.0 %collective-permute-start.76 = (bf16[2,4,128,256]{3,2,1,0:T(8,128)(2,1)S(1)}, bf16[2,4,128,256]{3,2,1,0:T(8,128)(2,1)}, u32[]{:S(2)}, u32[]{:S(2)}) collective-permute-start(bf16[2,4,128,256]{3,2,1,0:T(8,128)(2,1)S(1)} %copy-done.24), channel_id=1, source_target_pairs={{0,9},{1,8},{2,11},{3,10},{4,13},{5,12},{6,15},{7,14},{8,17},{9,16... | collective-permute-start | bytes 1572872 | tf_op jit(solution)/shard_map/ppermute | solution.py:39
  443.1 45.9 %collective-permute-start.42 = (bf16[2,4,128,256]{3,2,1,0:T(8,128)(2,1)}, bf16[2,4,128,256]{3,2,1,0:T(8,128)(2,1)}, u32[]{:S(2)}, u32[]{:S(2)}) collective-permute-start(bf16[2,4,128,256]{3,2,1,0:T(8,128)(2,1)} %get-tuple-element.137), channel_id=1, source_target_pairs={{0,7},{1,6},{2,1},{3,0},{4,3},{5,2},{6,5},{7,4},{8,15},{9,14},{10,... | collective-permute-start | bytes 1572872 | tf_op jit(solution)/shard_map/ppermute | solution.py:39
  443.3 45.7 %collective-permute-start.43 = (bf16[2,4,128,256]{3,2,1,0:T(8,128)(2,1)}, bf16[2,4,128,256]{3,2,1,0:T(8,128)(2,1)}, u32[]{:S(2)}, u32[]{:S(2)}) collective-permute-start(bf16[2,4,128,256]{3,2,1,0:T(8,128)(2,1)} %get-tuple-element.138), channel_id=1, source_target_pairs={{0,4},{1,5},{2,6},{3,7},{4,0},{5,1},{6,2},{7,3},{8,12},{9,13},{10,... | collective-permute-start | bytes 1572872 | tf_op jit(solution)/shard_map/ppermute | solution.py:39
  448.8 43.7 %collective-permute-start.44 = (bf16[2,4,128,256]{3,2,1,0:T(8,128)(2,1)}, bf16[2,4,128,256]{3,2,1,0:T(8,128)(2,1)}, u32[]{:S(2)}, u32[]{:S(2)}) collective-permute-start(bf16[2,4,128,256]{3,2,1,0:T(8,128)(2,1)} %get-tuple-element.139), channel_id=1, source_target_pairs={{0,5},{1,4},{2,7},{3,6},{4,1},{5,0},{6,3},{7,2},{8,13},{9,12},{10,... | collective-permute-start | bytes 1572872 | tf_op jit(solution)/shard_map/ppermute | solution.py:39
  448.8 43.7 %collective-permute-start.45 = (bf16[2,4,128,256]{3,2,1,0:T(8,128)(2,1)}, bf16[2,4,128,256]{3,2,1,0:T(8,128)(2,1)}, u32[]{:S(2)}, u32[]{:S(2)}) collective-permute-start(bf16[2,4,128,256]{3,2,1,0:T(8,128)(2,1)} %get-tuple-element.140), channel_id=1, source_target_pairs={{0,2},{1,3},{2,4},{3,5},{4,6},{5,7},{6,0},{7,1},{8,10},{9,11},{10,... | collective-permute-start | bytes 1572872 | tf_op jit(solution)/shard_map/ppermute | solution.py:39
  492.5 45.6 %collective-permute-start.62 = (bf16[2,4,128,256]{3,2,1,0:T(8,128)(2,1)}, bf16[2,4,128,256]{3,2,1,0:T(8,128)(2,1)}, u32[]{:S(2)}, u32[]{:S(2)}) collective-permute-start(bf16[2,4,128,256]{3,2,1,0:T(8,128)(2,1)} %get-tuple-element.161), channel_id=1, source_target_pairs={{0,7},{1,6},{2,1},{3,0},{4,3},{5,2},{6,5},{7,4},{8,15},{9,14},{10,... | collective-permute-start | bytes 1572872 | tf_op jit(solution)/shard_map/ppermute | solution.py:39
  492.5 48.5 %collective-permute-start.63 = (bf16[2,4,128,256]{3,2,1,0:T(8,128)(2,1)}, bf16[2,4,128,256]{3,2,1,0:T(8,128)(2,1)}, u32[]{:S(2)}, u32[]{:S(2)}) collective-permute-start(bf16[2,4,128,256]{3,2,1,0:T(8,128)(2,1)} %get-tuple-element.162), channel_id=1, source_target_pairs={{0,4},{1,5},{2,6},{3,7},{4,0},{5,1},{6,2},{7,3},{8,12},{9,13},{10,... | collective-permute-start | bytes 1572872 | tf_op jit(solution)/shard_map/ppermute | solution.py:39
  492.9 52.7 %collective-permute-start.64 = (bf16[2,4,128,256]{3,2,1,0:T(8,128)(2,1)}, bf16[2,4,128,256]{3,2,1,0:T(8,128)(2,1)}, u32[]{:S(2)}, u32[]{:S(2)}) collective-permute-start(bf16[2,4,128,256]{3,2,1,0:T(8,128)(2,1)} %get-tuple-element.163), channel_id=1, source_target_pairs={{0,5},{1,4},{2,7},{3,6},{4,1},{5,0},{6,3},{7,2},{8,13},{9,12},{10,... | collective-permute-start | bytes 1572872 | tf_op jit(solution)/shard_map/ppermute | solution.py:39
  495.5 51.3 %collective-permute-start.65 = (bf16[2,4,128,256]{3,2,1,0:T(8,128)(2,1)}, bf16[2,4,128,256]{3,2,1,0:T(8,128)(2,1)}, u32[]{:S(2)}, u32[]{:S(2)}) collective-permute-start(bf16[2,4,128,256]{3,2,1,0:T(8,128)(2,1)} %get-tuple-element.164), channel_id=1, source_target_pairs={{0,2},{1,3},{2,4},{3,5},{4,6},{5,7},{6,0},{7,1},{8,10},{9,11},{10,... | collective-permute-start | bytes 1572872 | tf_op jit(solution)/shard_map/ppermute | solution.py:39
  505.1 51.9 %collective-permute-start.66 = (bf16[2,4,128,256]{3,2,1,0:T(8,128)(2,1)}, bf16[2,4,128,256]{3,2,1,0:T(8,128)(2,1)}, u32[]{:S(2)}, u32[]{:S(2)}) collective-permute-start(bf16[2,4,128,256]{3,2,1,0:T(8,128)(2,1)} %get-tuple-element.165), channel_id=1, source_target_pairs={{0,3},{1,2},{2,5},{3,4},{4,7},{5,6},{6,1},{7,0},{8,11},{9,10},{10,... | collective-permute-start | bytes 1572872 | tf_op jit(solution)/shard_map/ppermute | solution.py:39
  (112 other events, 3282.7 us)
